TPU v7x, 512 devices: a whole 4x8x8 slice. The times are simulated.
512 devices in a mesh: section: 8 (over y_lo, core), tile: 64 (over y_hi, x, z).
Axes of the slice: x: 4, y: 8 (y_hi: 2, y_lo: 4; y = y_hi * 4 + y_lo), z: 8, core: 2. Of those that a mesh axis runs over, the one named last changes fastest.
Arguments:
- frames: bfloat16 [4, 128, 64, 256], P(None, None, 'tile'), may hold values from -6 to 6
- weights: bfloat16 [8, 9, 512, 256], P('section'), may hold values from -0.375 to 0.375
- gate_bias: float32 [8, 512], P('section'), may hold values from -3 to 3
- cotangent: bfloat16 [8, 4, 128, 64, 256], P('section', None, None, 'tile'), may hold values from -6 to 6
Outputs:
- hidden_seq: bfloat16 [8, 4, 128, 64, 256], P('section', None, None, 'tile')
- input_grads: bfloat16 [8, 4, 128, 64, 256], P('section', None, None, 'tile')
All inputs are finite; a program needn't handle non-finite values.
Results may differ from a plain program's by a relative error of at most 0.015.
Values may be sent and summed in bfloat16 or wider, within the bound.
A program may use at most 64 MiB of HBM per device.

v0:
```python
import jax
import jax.numpy as jnp
from jax import lax
from jax.sharding import PartitionSpec as P

TG = 8
TR = 16
TC = 16


def as_sent(value):
    return jax.tree.map(lambda a: a.astype(jnp.bfloat16) if a.dtype == jnp.float32 else a, value)


def from_behind(value, axis, steps):
    count = lax.axis_size(axis)
    initial, last = (max(0, -steps), min(count, count - steps))
    return lax.ppermute(value, axis, [(source, source + steps) for source in range(initial, last)])


def move_rims(piece, offset):
    return jax.tree.map(
        lambda part, own: part.astype(own.dtype), from_behind(as_sent(piece), "tile", offset), piece
    )


def move_grads(piece, offset):
    return jax.tree.map(
        lambda part, own: part.astype(own.dtype), from_behind(as_sent(piece), "tile", offset), piece
    )


def extend(field, mover, column_block):
    row_count = field.shape[-2]
    col_count = field.shape[-1]
    found = {}
    for delta_row in (-1, 0, 1):
        for delta_col in (-1, 0, 1):
            if delta_row == 0 and delta_col == 0:
                continue
            if delta_row == -1:
                row_part = field[..., row_count - 1 : row_count, :]
            elif delta_row == 1:
                row_part = field[..., 0:1, :]
            else:
                row_part = field
            if delta_col == -1:
                piece = row_part[..., col_count - 1 : col_count]
            elif delta_col == 1:
                piece = row_part[..., 0:1]
            else:
                piece = row_part
            received = mover(piece, -(delta_row * TG + delta_col))
            if delta_col != 0:
                valid = (column_block + delta_col >= 0) & (column_block + delta_col < TG)
                received = jnp.where(valid, received, jnp.zeros_like(received))
            found[delta_row, delta_col] = received
    upper = jnp.concatenate([found[-1, -1], found[-1, 0], found[-1, 1]], -1)
    middle = jnp.concatenate([found[0, -1], field, found[0, 1]], -1)
    lower = jnp.concatenate([found[1, -1], found[1, 0], found[1, 1]], -1)
    return jnp.concatenate([upper, middle, lower], -2)


def gate_terms(kernel, extended):
    row_count = extended.shape[1] - 2
    col_count = extended.shape[2] - 2
    summed = None
    for offset_row in range(3):
        for offset_col in range(3):
            window = extended[
                :, offset_row : offset_row + row_count, offset_col : offset_col + col_count
            ]
            window = window.reshape(extended.shape[0], row_count * col_count)
            product_term = jnp.dot(
                kernel[offset_row * 3 + offset_col], window, preferred_element_type=jnp.float32
            )
            summed = product_term if summed is None else summed + product_term
    return summed.reshape(kernel.shape[1], row_count, col_count)


def input_terms(kernel, extended):
    row_count = extended.shape[1] - 2
    col_count = extended.shape[2] - 2
    summed = None
    for offset_row in range(3):
        for offset_col in range(3):
            window = extended[
                :,
                2 - offset_row : 2 - offset_row + row_count,
                2 - offset_col : 2 - offset_col + col_count,
            ]
            window = window.reshape(extended.shape[0], row_count * col_count)
            product_term = lax.dot_general(
                kernel[offset_row * 3 + offset_col],
                window,
                (((0,), (0,)), ((), ())),
                preferred_element_type=jnp.float32,
            )
            summed = product_term if summed is None else summed + product_term
    return summed.reshape(kernel.shape[2], row_count, col_count)


def activate(preact):
    quarter = preact.shape[0] // 4
    return jnp.concatenate(
        [
            jax.nn.sigmoid(preact[: 2 * quarter]),
            jnp.tanh(preact[2 * quarter : 3 * quarter]),
            jax.nn.sigmoid(preact[3 * quarter :]),
        ],
        0,
    )


def state_grads(gate_values, cell_prev, cell_now, d_hidden, d_cell):
    quarter = gate_values.shape[0] // 4
    in_gate = gate_values[:quarter]
    forget = gate_values[quarter : 2 * quarter]
    cand_gate = gate_values[2 * quarter : 3 * quarter]
    out_gate = gate_values[3 * quarter :]
    tanh_cell = jnp.tanh(cell_now)
    d_out = d_hidden * tanh_cell
    d_total = d_cell + d_hidden * out_gate * (1.0 - tanh_cell * tanh_cell)
    d_gates = jnp.concatenate(
        [
            d_total * cand_gate * in_gate * (1.0 - in_gate),
            d_total * cell_prev * forget * (1.0 - forget),
            d_total * in_gate * (1.0 - cand_gate * cand_gate),
            d_out * out_gate * (1.0 - out_gate),
        ],
        0,
    ).astype(jnp.bfloat16)
    return (d_gates, d_total * forget)


def per_device(frames, weights, gate_bias, cotangent):
    kernel = weights[0]
    bias_col = gate_bias[0][:, None, None]
    step_count = frames.shape[0]
    width_ch = frames.shape[1]
    frames_tile = frames.reshape(step_count, width_ch, TR, TC)
    layer_cot = cotangent[0].reshape(step_count, width_ch, TR, TC)
    section_index = lax.axis_index("section")
    section_count = lax.axis_size("section")
    column_block = lax.axis_index("tile") % TG
    tick_count = step_count + section_count - 1
    plane = (width_ch, TR, TC)
    hidden_zero = jnp.zeros(plane, jnp.bfloat16)
    cell_zero = jnp.zeros(plane, jnp.float32)
    saved_start = jnp.zeros((step_count, 4 * width_ch, TR, TC), jnp.float32)
    hidden_start = jnp.zeros((step_count,) + plane, jnp.bfloat16)
    cell_start = jnp.zeros((step_count + 1,) + plane, jnp.float32)

    def forward_tick(tick_index, state_in):
        sent_now, hidden_now, cell_now, hidden_buf, cell_buf, saved_buf = state_in
        arrived = from_behind(sent_now, "section", 1)
        step_index = tick_index - section_index
        active = (step_index >= 0) & (step_index < step_count)
        slot_index = jnp.clip(step_index, 0, step_count - 1).astype(jnp.int32)
        frame_now = lax.dynamic_index_in_dim(frames_tile, slot_index, 0, keepdims=False)
        layer_in = jnp.where(section_index == 0, frame_now, arrived)
        extended = extend(jnp.concatenate([layer_in, hidden_now], 0), move_rims, column_block)

        def advance(inner):
            hidden_old, cell_old, hidden_acc, cell_acc, saved_acc = inner
            gate_values = activate(gate_terms(kernel, extended) + bias_col)
            cell_new = (
                gate_values[width_ch : 2 * width_ch] * cell_old
                + gate_values[:width_ch] * gate_values[2 * width_ch : 3 * width_ch]
            )
            hidden_new = (gate_values[3 * width_ch :] * jnp.tanh(cell_new)).astype(jnp.bfloat16)
            hidden_acc = lax.dynamic_update_index_in_dim(hidden_acc, hidden_new, slot_index, 0)
            cell_acc = lax.dynamic_update_index_in_dim(cell_acc, cell_new, slot_index + 1, 0)
            saved_acc = lax.dynamic_update_index_in_dim(saved_acc, gate_values, slot_index, 0)
            return (hidden_new, cell_new, hidden_acc, cell_acc, saved_acc)

        def forward_remain(inner):
            return inner

        hidden_now, cell_now, hidden_buf, cell_buf, saved_buf = lax.cond(
            active, advance, forward_remain, (hidden_now, cell_now, hidden_buf, cell_buf, saved_buf)
        )
        sent_now = hidden_now
        return (sent_now, hidden_now, cell_now, hidden_buf, cell_buf, saved_buf)

    forward_out = lax.fori_loop(
        0,
        tick_count,
        forward_tick,
        (hidden_zero, hidden_zero, cell_zero, hidden_start, cell_start, saved_start),
    )
    hidden_buf = forward_out[3]
    cell_buf = forward_out[4]
    saved_buf = forward_out[5]

    def backward_tick(tick_index, state_in):
        sent_grad, d_hidden_rec, d_cell, grad_buf = state_in
        arrived = from_behind(sent_grad, "section", -1)
        step_index = step_count - 1 - tick_index + (section_count - 1 - section_index)
        active = (step_index >= 0) & (step_index < step_count)
        slot_index = jnp.clip(step_index, 0, step_count - 1).astype(jnp.int32)
        gate_values = lax.dynamic_index_in_dim(saved_buf, slot_index, 0, keepdims=False)
        cell_prev = lax.dynamic_index_in_dim(cell_buf, slot_index, 0, keepdims=False)
        cell_now = lax.dynamic_index_in_dim(cell_buf, slot_index + 1, 0, keepdims=False)
        cot_now = lax.dynamic_index_in_dim(layer_cot, slot_index, 0, keepdims=False)
        d_hidden = cot_now.astype(jnp.float32) + arrived.astype(jnp.float32) + d_hidden_rec
        d_gates, d_cell_next = state_grads(gate_values, cell_prev, cell_now, d_hidden, d_cell)
        extended_grad = extend(d_gates, move_grads, column_block)

        def retreat(inner):
            grad_acc = inner[3]
            input_grad = input_terms(kernel, extended_grad)
            d_input = input_grad[:width_ch].astype(jnp.bfloat16)
            grad_acc = lax.dynamic_update_index_in_dim(grad_acc, d_input, slot_index, 0)
            return (d_input, input_grad[width_ch:], d_cell_next, grad_acc)

        def backward_remain(inner):
            return inner

        return lax.cond(
            active, retreat, backward_remain, (sent_grad, d_hidden_rec, d_cell, grad_buf)
        )

    backward_out = lax.fori_loop(
        0, tick_count, backward_tick, (hidden_zero, cell_zero, cell_zero, hidden_start)
    )
    hidden_out = hidden_buf.reshape(1, step_count, width_ch, 1, TR * TC)
    grad_out = backward_out[3].reshape(1, step_count, width_ch, 1, TR * TC)
    return (hidden_out, grad_out)


def solution(mesh):
    in_specs = (
        P(None, None, "tile", None),
        P("section", None, None, None),
        P("section", None),
        P("section", None, None, "tile", None),
    )
    out_specs = (P("section", None, None, "tile", None), P("section", None, None, "tile", None))
    return jax.shard_map(
        per_device, mesh=mesh, in_specs=in_specs, out_specs=out_specs, check_vma=False
    )
```

profile of v0, /device:TPU:6, one launch (start us, length us, event | category | flops | bytes accessed | tf_op | source)
XLA Modules:
  0.0 1204.4 jit_solution(2847220667644455643)
XLA Ops:
  5.3 571.7 %while.46 = (s32[]{:T(128)}, bf16[128,16,16]{0,2,1:T(8,128)(2,1)S(1)}, bf16[128,16,16]{0,2,1:T(8,128)(2,1)S(1)}, f32[128,16,16]{0,2,1:T(8,128)S(1)}, bf16[4,128,...) while((s32[]{:T(128)}, ...), condition=%wide.region_3.4_spmd, body=%wide.region_0.3_spmd.sunk | while | flops 608601088 | bytes 20960088 | solution.py:186
  8.0 11.8 collective-permute-start.1
  30.1 12.7 %collective-permute-start.6 = (bf16[256,1,1]{0,2,1:T(2,128)(2,1)S(1)}, bf16[256,1,1]{0,2,1:T(2,128)(2,1)S(1)}, u32[]{:S(2)}, u32[]{:S(2)}) collective-permute-start(bf16[256,1,1]{0,2,1:T(2,128)(2,1)S(1)} %get-tuple-element.1003), channel_id=1, source_target_pairs={{0,7},{1,8},{2,9},{3,10},{4,11},{5,12},{6,13},{7,14},{8,15},{9,16}... | collective-permute-start | bytes 1544 | tf_op jit(solution)/shard_map/while/body/eval_jaxpr/ppermute | solution.py:18
  44.1 8.4 collective-permute-start.7
  54.5 7.1 collective-permute-done.8
  81.7 12.5 %collective-permute-start.6 = (bf16[256,1,1]{0,2,1:T(2,128)(2,1)S(1)}, bf16[256,1,1]{0,2,1:T(2,128)(2,1)S(1)}, u32[]{:S(2)}, u32[]{:S(2)}) collective-permute-start(bf16[256,1,1]{0,2,1:T(2,128)(2,1)S(1)} %get-tuple-element.1003), channel_id=1, source_target_pairs={{0,7},{1,8},{2,9},{3,10},{4,11},{5,12},{6,13},{7,14},{8,15},{9,16}... | collective-permute-start | bytes 1544 | tf_op jit(solution)/shard_map/while/body/eval_jaxpr/ppermute | solution.py:18
  95.5 8.4 collective-permute-start.7
  133.2 12.5 %collective-permute-start.6 = (bf16[256,1,1]{0,2,1:T(2,128)(2,1)S(1)}, bf16[256,1,1]{0,2,1:T(2,128)(2,1)S(1)}, u32[]{:S(2)}, u32[]{:S(2)}) collective-permute-start(bf16[256,1,1]{0,2,1:T(2,128)(2,1)S(1)} %get-tuple-element.1003), channel_id=1, source_target_pairs={{0,7},{1,8},{2,9},{3,10},{4,11},{5,12},{6,13},{7,14},{8,15},{9,16}... | collective-permute-start | bytes 1544 | tf_op jit(solution)/shard_map/while/body/eval_jaxpr/ppermute | solution.py:18
  147.0 8.4 collective-permute-start.7
  184.6 12.5 %collective-permute-start.6 = (bf16[256,1,1]{0,2,1:T(2,128)(2,1)S(1)}, bf16[256,1,1]{0,2,1:T(2,128)(2,1)S(1)}, u32[]{:S(2)}, u32[]{:S(2)}) collective-permute-start(bf16[256,1,1]{0,2,1:T(2,128)(2,1)S(1)} %get-tuple-element.1003), channel_id=1, source_target_pairs={{0,7},{1,8},{2,9},{3,10},{4,11},{5,12},{6,13},{7,14},{8,15},{9,16}... | collective-permute-start | bytes 1544 | tf_op jit(solution)/shard_map/while/body/eval_jaxpr/ppermute | solution.py:18
  198.5 8.4 collective-permute-start.7
  236.1 12.5 %collective-permute-start.6 = (bf16[256,1,1]{0,2,1:T(2,128)(2,1)S(1)}, bf16[256,1,1]{0,2,1:T(2,128)(2,1)S(1)}, u32[]{:S(2)}, u32[]{:S(2)}) collective-permute-start(bf16[256,1,1]{0,2,1:T(2,128)(2,1)S(1)} %get-tuple-element.1003), channel_id=1, source_target_pairs={{0,7},{1,8},{2,9},{3,10},{4,11},{5,12},{6,13},{7,14},{8,15},{9,16}... | collective-permute-start | bytes 1544 | tf_op jit(solution)/shard_map/while/body/eval_jaxpr/ppermute | solution.py:18
  249.9 8.4 collective-permute-start.7
  267.9 9.7 collective-permute-start
  290.9 12.6 %collective-permute-start.6 = (bf16[256,1,1]{0,2,1:T(2,128)(2,1)S(1)}, bf16[256,1,1]{0,2,1:T(2,128)(2,1)S(1)}, u32[]{:S(2)}, u32[]{:S(2)}) collective-permute-start(bf16[256,1,1]{0,2,1:T(2,128)(2,1)S(1)} %get-tuple-element.1003), channel_id=1, source_target_pairs={{0,7},{1,8},{2,9},{3,10},{4,11},{5,12},{6,13},{7,14},{8,15},{9,16}... | collective-permute-start | bytes 1544 | tf_op jit(solution)/shard_map/while/body/eval_jaxpr/ppermute | solution.py:18
  304.8 8.4 collective-permute-start.7
  315.4 6.9 collective-permute-done.8
  340.7 12.6 %collective-permute-start.6 = (bf16[256,1,1]{0,2,1:T(2,128)(2,1)S(1)}, bf16[256,1,1]{0,2,1:T(2,128)(2,1)S(1)}, u32[]{:S(2)}, u32[]{:S(2)}) collective-permute-start(bf16[256,1,1]{0,2,1:T(2,128)(2,1)S(1)} %get-tuple-element.1003), channel_id=1, source_target_pairs={{0,7},{1,8},{2,9},{3,10},{4,11},{5,12},{6,13},{7,14},{8,15},{9,16}... | collective-permute-start | bytes 1544 | tf_op jit(solution)/shard_map/while/body/eval_jaxpr/ppermute | solution.py:18
  354.6 8.4 collective-permute-start.7
  365.2 6.9 collective-permute-done.8
  372.6 9.7 collective-permute-start
  395.6 12.6 %collective-permute-start.6 = (bf16[256,1,1]{0,2,1:T(2,128)(2,1)S(1)}, bf16[256,1,1]{0,2,1:T(2,128)(2,1)S(1)}, u32[]{:S(2)}, u32[]{:S(2)}) collective-permute-start(bf16[256,1,1]{0,2,1:T(2,128)(2,1)S(1)} %get-tuple-element.1003), channel_id=1, source_target_pairs={{0,7},{1,8},{2,9},{3,10},{4,11},{5,12},{6,13},{7,14},{8,15},{9,16}... | collective-permute-start | bytes 1544 | tf_op jit(solution)/shard_map/while/body/eval_jaxpr/ppermute | solution.py:18
  409.5 8.4 collective-permute-start.7
  445.5 12.6 %collective-permute-start.6 = (bf16[256,1,1]{0,2,1:T(2,128)(2,1)S(1)}, bf16[256,1,1]{0,2,1:T(2,128)(2,1)S(1)}, u32[]{:S(2)}, u32[]{:S(2)}) collective-permute-start(bf16[256,1,1]{0,2,1:T(2,128)(2,1)S(1)} %get-tuple-element.1003), channel_id=1, source_target_pairs={{0,7},{1,8},{2,9},{3,10},{4,11},{5,12},{6,13},{7,14},{8,15},{9,16}... | collective-permute-start | bytes 1544 | tf_op jit(solution)/shard_map/while/body/eval_jaxpr/ppermute | solution.py:18
  459.3 8.4 collective-permute-start.7
  495.3 12.6 %collective-permute-start.6 = (bf16[256,1,1]{0,2,1:T(2,128)(2,1)S(1)}, bf16[256,1,1]{0,2,1:T(2,128)(2,1)S(1)}, u32[]{:S(2)}, u32[]{:S(2)}) collective-permute-start(bf16[256,1,1]{0,2,1:T(2,128)(2,1)S(1)} %get-tuple-element.1003), channel_id=1, source_target_pairs={{0,7},{1,8},{2,9},{3,10},{4,11},{5,12},{6,13},{7,14},{8,15},{9,16}... | collective-permute-start | bytes 1544 | tf_op jit(solution)/shard_map/while/body/eval_jaxpr/ppermute | solution.py:18
  509.2 8.4 collective-permute-start.7
  545.2 12.6 %collective-permute-start.6 = (bf16[256,1,1]{0,2,1:T(2,128)(2,1)S(1)}, bf16[256,1,1]{0,2,1:T(2,128)(2,1)S(1)}, u32[]{:S(2)}, u32[]{:S(2)}) collective-permute-start(bf16[256,1,1]{0,2,1:T(2,128)(2,1)S(1)} %get-tuple-element.1003), channel_id=1, source_target_pairs={{0,7},{1,8},{2,9},{3,10},{4,11},{5,12},{6,13},{7,14},{8,15},{9,16}... | collective-permute-start | bytes 1544 | tf_op jit(solution)/shard_map/while/body/eval_jaxpr/ppermute | solution.py:18
  559.0 8.4 collective-permute-start.7
  580.6 623.0 %while.47 = (s32[]{:T(128)}, bf16[128,16,16]{0,2,1:T(8,128)(2,1)}, f32[128,16,16]{0,2,1:T(8,128)S(1)}, f32[128,16,16]{0,2,1:T(8,128)S(1)}, bf16[4,128,16,16]{1,3...) while((s32[]{:T(128)}, bf16[128,16,16]{0,2,1:T(8,128)(2,1)}, ...), condition=%wide.region_7.8_spmd, body=%wide.region_4.7_spmd.sunk | while | flops 612304896 | bytes 18916232 | solution.py:224
  601.8 12.6 %collective-permute-start.15 = (bf16[512,1,1]{0,2,1:T(2,128)(2,1)S(1)}, bf16[512,1,1]{0,2,1:T(2,128)(2,1)S(1)}, u32[]{:S(2)}, u32[]{:S(2)}) collective-permute-start(bf16[512,1,1]{0,2,1:T(2,128)(2,1)S(1)} %get-tuple-element.1033), channel_id=1, source_target_pairs={{0,7},{1,8},{2,9},{3,10},{4,11},{5,12},{6,13},{7,14},{8,15},{9,16}... | collective-permute-start | bytes 3080 | tf_op jit(solution)/shard_map/while/body/eval_jaxpr/ppermute | solution.py:18
  615.7 8.4 collective-permute-start.16
  626.3 6.9 collective-permute-done.17
  655.9 12.6 %collective-permute-start.15 = (bf16[512,1,1]{0,2,1:T(2,128)(2,1)S(1)}, bf16[512,1,1]{0,2,1:T(2,128)(2,1)S(1)}, u32[]{:S(2)}, u32[]{:S(2)}) collective-permute-start(bf16[512,1,1]{0,2,1:T(2,128)(2,1)S(1)} %get-tuple-element.1033), channel_id=1, source_target_pairs={{0,7},{1,8},{2,9},{3,10},{4,11},{5,12},{6,13},{7,14},{8,15},{9,16}... | collective-permute-start | bytes 3080 | tf_op jit(solution)/shard_map/while/body/eval_jaxpr/ppermute | solution.py:18
  669.8 8.4 collective-permute-start.16
  680.4 6.9 collective-permute-done.17
  707.7 12.6 %collective-permute-start.15 = (bf16[512,1,1]{0,2,1:T(2,128)(2,1)S(1)}, bf16[512,1,1]{0,2,1:T(2,128)(2,1)S(1)}, u32[]{:S(2)}, u32[]{:S(2)}) collective-permute-start(bf16[512,1,1]{0,2,1:T(2,128)(2,1)S(1)} %get-tuple-element.1033), channel_id=1, source_target_pairs={{0,7},{1,8},{2,9},{3,10},{4,11},{5,12},{6,13},{7,14},{8,15},{9,16}... | collective-permute-start | bytes 3080 | tf_op jit(solution)/shard_map/while/body/eval_jaxpr/ppermute | solution.py:18
  721.5 8.4 collective-permute-start.16
  732.1 6.9 collective-permute-done.17
  759.6 12.6 %collective-permute-start.15 = (bf16[512,1,1]{0,2,1:T(2,128)(2,1)S(1)}, bf16[512,1,1]{0,2,1:T(2,128)(2,1)S(1)}, u32[]{:S(2)}, u32[]{:S(2)}) collective-permute-start(bf16[512,1,1]{0,2,1:T(2,128)(2,1)S(1)} %get-tuple-element.1033), channel_id=1, source_target_pairs={{0,7},{1,8},{2,9},{3,10},{4,11},{5,12},{6,13},{7,14},{8,15},{9,16}... | collective-permute-start | bytes 3080 | tf_op jit(solution)/shard_map/while/body/eval_jaxpr/ppermute | solution.py:18
  773.4 8.4 collective-permute-start.16
  784.0 6.9 collective-permute-done.17
  811.3 12.6 %collective-permute-start.15 = (bf16[512,1,1]{0,2,1:T(2,128)(2,1)S(1)}, bf16[512,1,1]{0,2,1:T(2,128)(2,1)S(1)}, u32[]{:S(2)}, u32[]{:S(2)}) collective-permute-start(bf16[512,1,1]{0,2,1:T(2,128)(2,1)S(1)} %get-tuple-element.1033), channel_id=1, source_target_pairs={{0,7},{1,8},{2,9},{3,10},{4,11},{5,12},{6,13},{7,14},{8,15},{9,16}... | collective-permute-start | bytes 3080 | tf_op jit(solution)/shard_map/while/body/eval_jaxpr/ppermute | solution.py:18
  825.2 8.4 collective-permute-start.16
  835.8 6.9 collective-permute-done.17
  863.2 12.6 %collective-permute-start.15 = (bf16[512,1,1]{0,2,1:T(2,128)(2,1)S(1)}, bf16[512,1,1]{0,2,1:T(2,128)(2,1)S(1)}, u32[]{:S(2)}, u32[]{:S(2)}) collective-permute-start(bf16[512,1,1]{0,2,1:T(2,128)(2,1)S(1)} %get-tuple-element.1033), channel_id=1, source_target_pairs={{0,7},{1,8},{2,9},{3,10},{4,11},{5,12},{6,13},{7,14},{8,15},{9,16}... | collective-permute-start | bytes 3080 | tf_op jit(solution)/shard_map/while/body/eval_jaxpr/ppermute | solution.py:18
  877.1 8.4 collective-permute-start.16
  887.7 6.9 collective-permute-done.17
  915.0 12.6 %collective-permute-start.15 = (bf16[512,1,1]{0,2,1:T(2,128)(2,1)S(1)}, bf16[512,1,1]{0,2,1:T(2,128)(2,1)S(1)}, u32[]{:S(2)}, u32[]{:S(2)}) collective-permute-start(bf16[512,1,1]{0,2,1:T(2,128)(2,1)S(1)} %get-tuple-element.1033), channel_id=1, source_target_pairs={{0,7},{1,8},{2,9},{3,10},{4,11},{5,12},{6,13},{7,14},{8,15},{9,16}... | collective-permute-start | bytes 3080 | tf_op jit(solution)/shard_map/while/body/eval_jaxpr/ppermute | solution.py:18
  928.9 8.4 collective-permute-start.16
  939.5 6.9 collective-permute-done.17
  948.4 32.4 %collective-permute-done.9 = bf16[128,16,16]{0,2,1:T(8,128)(2,1)S(1)} collective-permute-done((bf16[128,16,16]{0,2,1:T(8,128)(2,1)}, bf16[128,16,16]{0,2,1:T(8,128)(2,1)S(1)}, u32[]{:S(2)}, u32[]{:S(2)}) %collective-permute-start.9) | collective-permute-done | bytes 65568 | tf_op jit(solution)/shard_map/while/body/eval_jaxpr/ppermute | solution.py:18
  996.4 12.6 %collective-permute-start.15 = (bf16[512,1,1]{0,2,1:T(2,128)(2,1)S(1)}, bf16[512,1,1]{0,2,1:T(2,128)(2,1)S(1)}, u32[]{:S(2)}, u32[]{:S(2)}) collective-permute-start(bf16[512,1,1]{0,2,1:T(2,128)(2,1)S(1)} %get-tuple-element.1033), channel_id=1, source_target_pairs={{0,7},{1,8},{2,9},{3,10},{4,11},{5,12},{6,13},{7,14},{8,15},{9,16}... | collective-permute-start | bytes 3080 | tf_op jit(solution)/shard_map/while/body/eval_jaxpr/ppermute | solution.py:18
  1010.3 8.4 collective-permute-start.16
  1020.9 6.9 collective-permute-done.17
  1053.1 12.6 %collective-permute-start.15 = (bf16[512,1,1]{0,2,1:T(2,128)(2,1)S(1)}, bf16[512,1,1]{0,2,1:T(2,128)(2,1)S(1)}, u32[]{:S(2)}, u32[]{:S(2)}) collective-permute-start(bf16[512,1,1]{0,2,1:T(2,128)(2,1)S(1)} %get-tuple-element.1033), channel_id=1, source_target_pairs={{0,7},{1,8},{2,9},{3,10},{4,11},{5,12},{6,13},{7,14},{8,15},{9,16}... | collective-permute-start | bytes 3080 | tf_op jit(solution)/shard_map/while/body/eval_jaxpr/ppermute | solution.py:18
  1067.0 8.4 collective-permute-start.16
  1077.6 6.9 collective-permute-done.17
  1109.8 12.6 %collective-permute-start.15 = (bf16[512,1,1]{0,2,1:T(2,128)(2,1)S(1)}, bf16[512,1,1]{0,2,1:T(2,128)(2,1)S(1)}, u32[]{:S(2)}, u32[]{:S(2)}) collective-permute-start(bf16[512,1,1]{0,2,1:T(2,128)(2,1)S(1)} %get-tuple-element.1033), channel_id=1, source_target_pairs={{0,7},{1,8},{2,9},{3,10},{4,11},{5,12},{6,13},{7,14},{8,15},{9,16}... | collective-permute-start | bytes 3080 | tf_op jit(solution)/shard_map/while/body/eval_jaxpr/ppermute | solution.py:18
  1123.7 8.4 collective-permute-start.16
  1134.3 6.9 collective-permute-done.17
  1166.6 12.6 %collective-permute-start.15 = (bf16[512,1,1]{0,2,1:T(2,128)(2,1)S(1)}, bf16[512,1,1]{0,2,1:T(2,128)(2,1)S(1)}, u32[]{:S(2)}, u32[]{:S(2)}) collective-permute-start(bf16[512,1,1]{0,2,1:T(2,128)(2,1)S(1)} %get-tuple-element.1033), channel_id=1, source_target_pairs={{0,7},{1,8},{2,9},{3,10},{4,11},{5,12},{6,13},{7,14},{8,15},{9,16}... | collective-permute-start | bytes 3080 | tf_op jit(solution)/shard_map/while/body/eval_jaxpr/ppermute | solution.py:18
  1180.4 8.4 collective-permute-start.16
  1191.0 6.9 collective-permute-done.17
  (802 shorter events, 615.4 us)
Async XLA Ops:
  19.8 42.0 %collective-permute-start.2 = (bf16[256,1,16]{0,2,1:T(8,128)(2,1)S(1)}, bf16[256,1,16]{0,2,1:T(8,128)(2,1)S(1)}, u32[]{:S(2)}, u32[]{:S(2)}) collective-permute-start(bf16[256,1,16]{0,2,1:T(8,128)(2,1)S(1)} %get-tuple-element.999), channel_id=1, source_target_pairs={{8,0},{9,1},{10,2},{11,3},{12,4},{13,5},{14,6},{15,7},{16,8},{17,9... | collective-permute-start | bytes 24584 | tf_op jit(solution)/shard_map/while/body/eval_jaxpr/ppermute | solution.py:18
  23.7 38.0 %collective-permute-start.4 = (bf16[256,16,1]{0,2,1:T(2,128)(2,1)S(1)}, bf16[256,16,1]{0,2,1:T(2,128)(2,1)S(1)}, u32[]{:S(2)}, u32[]{:S(2)}) collective-permute-start(bf16[256,16,1]{0,2,1:T(2,128)(2,1)S(1)} %get-tuple-element.1001), channel_id=1, source_target_pairs={{1,0},{2,1},{3,2},{4,3},{5,4},{6,5},{7,6},{8,7},{9,8},{10,9},{11,1... | collective-permute-start | bytes 24584 | tf_op jit(solution)/shard_map/while/body/eval_jaxpr/ppermute | solution.py:18
  71.3 42.0 %collective-permute-start.2 = (bf16[256,1,16]{0,2,1:T(8,128)(2,1)S(1)}, bf16[256,1,16]{0,2,1:T(8,128)(2,1)S(1)}, u32[]{:S(2)}, u32[]{:S(2)}) collective-permute-start(bf16[256,1,16]{0,2,1:T(8,128)(2,1)S(1)} %get-tuple-element.999), channel_id=1, source_target_pairs={{8,0},{9,1},{10,2},{11,3},{12,4},{13,5},{14,6},{15,7},{16,8},{17,9... | collective-permute-start | bytes 24584 | tf_op jit(solution)/shard_map/while/body/eval_jaxpr/ppermute | solution.py:18
  75.1 38.0 %collective-permute-start.4 = (bf16[256,16,1]{0,2,1:T(2,128)(2,1)S(1)}, bf16[256,16,1]{0,2,1:T(2,128)(2,1)S(1)}, u32[]{:S(2)}, u32[]{:S(2)}) collective-permute-start(bf16[256,16,1]{0,2,1:T(2,128)(2,1)S(1)} %get-tuple-element.1001), channel_id=1, source_target_pairs={{1,0},{2,1},{3,2},{4,3},{5,4},{6,5},{7,6},{8,7},{9,8},{10,9},{11,1... | collective-permute-start | bytes 24584 | tf_op jit(solution)/shard_map/while/body/eval_jaxpr/ppermute | solution.py:18
  77.0 36.1 %collective-permute-start.5 = (bf16[256,16,1]{0,2,1:T(2,128)(2,1)S(1)}, bf16[256,16,1]{0,2,1:T(2,128)(2,1)S(1)}, u32[]{:S(2)}, u32[]{:S(2)}) collective-permute-start(bf16[256,16,1]{0,2,1:T(2,128)(2,1)S(1)} %get-tuple-element.1002), channel_id=1, source_target_pairs={{0,1},{1,2},{2,3},{3,4},{4,5},{5,6},{6,7},{7,8},{8,9},{9,10},{10,1... | collective-permute-start | bytes 24584 | tf_op jit(solution)/shard_map/while/body/eval_jaxpr/ppermute | solution.py:18
  122.7 42.0 %collective-permute-start.2 = (bf16[256,1,16]{0,2,1:T(8,128)(2,1)S(1)}, bf16[256,1,16]{0,2,1:T(8,128)(2,1)S(1)}, u32[]{:S(2)}, u32[]{:S(2)}) collective-permute-start(bf16[256,1,16]{0,2,1:T(8,128)(2,1)S(1)} %get-tuple-element.999), channel_id=1, source_target_pairs={{8,0},{9,1},{10,2},{11,3},{12,4},{13,5},{14,6},{15,7},{16,8},{17,9... | collective-permute-start | bytes 24584 | tf_op jit(solution)/shard_map/while/body/eval_jaxpr/ppermute | solution.py:18
  126.6 38.0 %collective-permute-start.4 = (bf16[256,16,1]{0,2,1:T(2,128)(2,1)S(1)}, bf16[256,16,1]{0,2,1:T(2,128)(2,1)S(1)}, u32[]{:S(2)}, u32[]{:S(2)}) collective-permute-start(bf16[256,16,1]{0,2,1:T(2,128)(2,1)S(1)} %get-tuple-element.1001), channel_id=1, source_target_pairs={{1,0},{2,1},{3,2},{4,3},{5,4},{6,5},{7,6},{8,7},{9,8},{10,9},{11,1... | collective-permute-start | bytes 24584 | tf_op jit(solution)/shard_map/while/body/eval_jaxpr/ppermute | solution.py:18
  128.5 36.1 %collective-permute-start.5 = (bf16[256,16,1]{0,2,1:T(2,128)(2,1)S(1)}, bf16[256,16,1]{0,2,1:T(2,128)(2,1)S(1)}, u32[]{:S(2)}, u32[]{:S(2)}) collective-permute-start(bf16[256,16,1]{0,2,1:T(2,128)(2,1)S(1)} %get-tuple-element.1002), channel_id=1, source_target_pairs={{0,1},{1,2},{2,3},{3,4},{4,5},{5,6},{6,7},{7,8},{8,9},{9,10},{10,1... | collective-permute-start | bytes 24584 | tf_op jit(solution)/shard_map/while/body/eval_jaxpr/ppermute | solution.py:18
  174.2 42.0 %collective-permute-start.2 = (bf16[256,1,16]{0,2,1:T(8,128)(2,1)S(1)}, bf16[256,1,16]{0,2,1:T(8,128)(2,1)S(1)}, u32[]{:S(2)}, u32[]{:S(2)}) collective-permute-start(bf16[256,1,16]{0,2,1:T(8,128)(2,1)S(1)} %get-tuple-element.999), channel_id=1, source_target_pairs={{8,0},{9,1},{10,2},{11,3},{12,4},{13,5},{14,6},{15,7},{16,8},{17,9... | collective-permute-start | bytes 24584 | tf_op jit(solution)/shard_map/while/body/eval_jaxpr/ppermute | solution.py:18
  178.0 38.0 %collective-permute-start.4 = (bf16[256,16,1]{0,2,1:T(2,128)(2,1)S(1)}, bf16[256,16,1]{0,2,1:T(2,128)(2,1)S(1)}, u32[]{:S(2)}, u32[]{:S(2)}) collective-permute-start(bf16[256,16,1]{0,2,1:T(2,128)(2,1)S(1)} %get-tuple-element.1001), channel_id=1, source_target_pairs={{1,0},{2,1},{3,2},{4,3},{5,4},{6,5},{7,6},{8,7},{9,8},{10,9},{11,1... | collective-permute-start | bytes 24584 | tf_op jit(solution)/shard_map/while/body/eval_jaxpr/ppermute | solution.py:18
  180.0 36.1 %collective-permute-start.5 = (bf16[256,16,1]{0,2,1:T(2,128)(2,1)S(1)}, bf16[256,16,1]{0,2,1:T(2,128)(2,1)S(1)}, u32[]{:S(2)}, u32[]{:S(2)}) collective-permute-start(bf16[256,16,1]{0,2,1:T(2,128)(2,1)S(1)} %get-tuple-element.1002), channel_id=1, source_target_pairs={{0,1},{1,2},{2,3},{3,4},{4,5},{5,6},{6,7},{7,8},{8,9},{9,10},{10,1... | collective-permute-start | bytes 24584 | tf_op jit(solution)/shard_map/while/body/eval_jaxpr/ppermute | solution.py:18
  225.6 42.0 %collective-permute-start.2 = (bf16[256,1,16]{0,2,1:T(8,128)(2,1)S(1)}, bf16[256,1,16]{0,2,1:T(8,128)(2,1)S(1)}, u32[]{:S(2)}, u32[]{:S(2)}) collective-permute-start(bf16[256,1,16]{0,2,1:T(8,128)(2,1)S(1)} %get-tuple-element.999), channel_id=1, source_target_pairs={{8,0},{9,1},{10,2},{11,3},{12,4},{13,5},{14,6},{15,7},{16,8},{17,9... | collective-permute-start | bytes 24584 | tf_op jit(solution)/shard_map/while/body/eval_jaxpr/ppermute | solution.py:18
  229.5 38.0 %collective-permute-start.4 = (bf16[256,16,1]{0,2,1:T(2,128)(2,1)S(1)}, bf16[256,16,1]{0,2,1:T(2,128)(2,1)S(1)}, u32[]{:S(2)}, u32[]{:S(2)}) collective-permute-start(bf16[256,16,1]{0,2,1:T(2,128)(2,1)S(1)} %get-tuple-element.1001), channel_id=1, source_target_pairs={{1,0},{2,1},{3,2},{4,3},{5,4},{6,5},{7,6},{8,7},{9,8},{10,9},{11,1... | collective-permute-start | bytes 24584 | tf_op jit(solution)/shard_map/while/body/eval_jaxpr/ppermute | solution.py:18
  231.4 36.1 %collective-permute-start.5 = (bf16[256,16,1]{0,2,1:T(2,128)(2,1)S(1)}, bf16[256,16,1]{0,2,1:T(2,128)(2,1)S(1)}, u32[]{:S(2)}, u32[]{:S(2)}) collective-permute-start(bf16[256,16,1]{0,2,1:T(2,128)(2,1)S(1)} %get-tuple-element.1002), channel_id=1, source_target_pairs={{0,1},{1,2},{2,3},{3,4},{4,5},{5,6},{6,7},{7,8},{8,9},{9,10},{10,1... | collective-permute-start | bytes 24584 | tf_op jit(solution)/shard_map/while/body/eval_jaxpr/ppermute | solution.py:18
  280.5 42.0 %collective-permute-start.2 = (bf16[256,1,16]{0,2,1:T(8,128)(2,1)S(1)}, bf16[256,1,16]{0,2,1:T(8,128)(2,1)S(1)}, u32[]{:S(2)}, u32[]{:S(2)}) collective-permute-start(bf16[256,1,16]{0,2,1:T(8,128)(2,1)S(1)} %get-tuple-element.999), channel_id=1, source_target_pairs={{8,0},{9,1},{10,2},{11,3},{12,4},{13,5},{14,6},{15,7},{16,8},{17,9... | collective-permute-start | bytes 24584 | tf_op jit(solution)/shard_map/while/body/eval_jaxpr/ppermute | solution.py:18
  284.4 38.0 %collective-permute-start.4 = (bf16[256,16,1]{0,2,1:T(2,128)(2,1)S(1)}, bf16[256,16,1]{0,2,1:T(2,128)(2,1)S(1)}, u32[]{:S(2)}, u32[]{:S(2)}) collective-permute-start(bf16[256,16,1]{0,2,1:T(2,128)(2,1)S(1)} %get-tuple-element.1001), channel_id=1, source_target_pairs={{1,0},{2,1},{3,2},{4,3},{5,4},{6,5},{7,6},{8,7},{9,8},{10,9},{11,1... | collective-permute-start | bytes 24584 | tf_op jit(solution)/shard_map/while/body/eval_jaxpr/ppermute | solution.py:18
  286.3 36.1 %collective-permute-start.5 = (bf16[256,16,1]{0,2,1:T(2,128)(2,1)S(1)}, bf16[256,16,1]{0,2,1:T(2,128)(2,1)S(1)}, u32[]{:S(2)}, u32[]{:S(2)}) collective-permute-start(bf16[256,16,1]{0,2,1:T(2,128)(2,1)S(1)} %get-tuple-element.1002), channel_id=1, source_target_pairs={{0,1},{1,2},{2,3},{3,4},{4,5},{5,6},{6,7},{7,8},{8,9},{9,10},{10,1... | collective-permute-start | bytes 24584 | tf_op jit(solution)/shard_map/while/body/eval_jaxpr/ppermute | solution.py:18
  330.3 42.0 %collective-permute-start.2 = (bf16[256,1,16]{0,2,1:T(8,128)(2,1)S(1)}, bf16[256,1,16]{0,2,1:T(8,128)(2,1)S(1)}, u32[]{:S(2)}, u32[]{:S(2)}) collective-permute-start(bf16[256,1,16]{0,2,1:T(8,128)(2,1)S(1)} %get-tuple-element.999), channel_id=1, source_target_pairs={{8,0},{9,1},{10,2},{11,3},{12,4},{13,5},{14,6},{15,7},{16,8},{17,9... | collective-permute-start | bytes 24584 | tf_op jit(solution)/shard_map/while/body/eval_jaxpr/ppermute | solution.py:18
  334.2 38.0 %collective-permute-start.4 = (bf16[256,16,1]{0,2,1:T(2,128)(2,1)S(1)}, bf16[256,16,1]{0,2,1:T(2,128)(2,1)S(1)}, u32[]{:S(2)}, u32[]{:S(2)}) collective-permute-start(bf16[256,16,1]{0,2,1:T(2,128)(2,1)S(1)} %get-tuple-element.1001), channel_id=1, source_target_pairs={{1,0},{2,1},{3,2},{4,3},{5,4},{6,5},{7,6},{8,7},{9,8},{10,9},{11,1... | collective-permute-start | bytes 24584 | tf_op jit(solution)/shard_map/while/body/eval_jaxpr/ppermute | solution.py:18
  336.1 36.1 %collective-permute-start.5 = (bf16[256,16,1]{0,2,1:T(2,128)(2,1)S(1)}, bf16[256,16,1]{0,2,1:T(2,128)(2,1)S(1)}, u32[]{:S(2)}, u32[]{:S(2)}) collective-permute-start(bf16[256,16,1]{0,2,1:T(2,128)(2,1)S(1)} %get-tuple-element.1002), channel_id=1, source_target_pairs={{0,1},{1,2},{2,3},{3,4},{4,5},{5,6},{6,7},{7,8},{8,9},{9,10},{10,1... | collective-permute-start | bytes 24584 | tf_op jit(solution)/shard_map/while/body/eval_jaxpr/ppermute | solution.py:18
  385.2 42.0 %collective-permute-start.2 = (bf16[256,1,16]{0,2,1:T(8,128)(2,1)S(1)}, bf16[256,1,16]{0,2,1:T(8,128)(2,1)S(1)}, u32[]{:S(2)}, u32[]{:S(2)}) collective-permute-start(bf16[256,1,16]{0,2,1:T(8,128)(2,1)S(1)} %get-tuple-element.999), channel_id=1, source_target_pairs={{8,0},{9,1},{10,2},{11,3},{12,4},{13,5},{14,6},{15,7},{16,8},{17,9... | collective-permute-start | bytes 24584 | tf_op jit(solution)/shard_map/while/body/eval_jaxpr/ppermute | solution.py:18
  389.1 38.0 %collective-permute-start.4 = (bf16[256,16,1]{0,2,1:T(2,128)(2,1)S(1)}, bf16[256,16,1]{0,2,1:T(2,128)(2,1)S(1)}, u32[]{:S(2)}, u32[]{:S(2)}) collective-permute-start(bf16[256,16,1]{0,2,1:T(2,128)(2,1)S(1)} %get-tuple-element.1001), channel_id=1, source_target_pairs={{1,0},{2,1},{3,2},{4,3},{5,4},{6,5},{7,6},{8,7},{9,8},{10,9},{11,1... | collective-permute-start | bytes 24584 | tf_op jit(solution)/shard_map/while/body/eval_jaxpr/ppermute | solution.py:18
  391.0 36.1 %collective-permute-start.5 = (bf16[256,16,1]{0,2,1:T(2,128)(2,1)S(1)}, bf16[256,16,1]{0,2,1:T(2,128)(2,1)S(1)}, u32[]{:S(2)}, u32[]{:S(2)}) collective-permute-start(bf16[256,16,1]{0,2,1:T(2,128)(2,1)S(1)} %get-tuple-element.1002), channel_id=1, source_target_pairs={{0,1},{1,2},{2,3},{3,4},{4,5},{5,6},{6,7},{7,8},{8,9},{9,10},{10,1... | collective-permute-start | bytes 24584 | tf_op jit(solution)/shard_map/while/body/eval_jaxpr/ppermute | solution.py:18
  435.0 42.0 %collective-permute-start.2 = (bf16[256,1,16]{0,2,1:T(8,128)(2,1)S(1)}, bf16[256,1,16]{0,2,1:T(8,128)(2,1)S(1)}, u32[]{:S(2)}, u32[]{:S(2)}) collective-permute-start(bf16[256,1,16]{0,2,1:T(8,128)(2,1)S(1)} %get-tuple-element.999), channel_id=1, source_target_pairs={{8,0},{9,1},{10,2},{11,3},{12,4},{13,5},{14,6},{15,7},{16,8},{17,9... | collective-permute-start | bytes 24584 | tf_op jit(solution)/shard_map/while/body/eval_jaxpr/ppermute | solution.py:18
  438.9 38.0 %collective-permute-start.4 = (bf16[256,16,1]{0,2,1:T(2,128)(2,1)S(1)}, bf16[256,16,1]{0,2,1:T(2,128)(2,1)S(1)}, u32[]{:S(2)}, u32[]{:S(2)}) collective-permute-start(bf16[256,16,1]{0,2,1:T(2,128)(2,1)S(1)} %get-tuple-element.1001), channel_id=1, source_target_pairs={{1,0},{2,1},{3,2},{4,3},{5,4},{6,5},{7,6},{8,7},{9,8},{10,9},{11,1... | collective-permute-start | bytes 24584 | tf_op jit(solution)/shard_map/while/body/eval_jaxpr/ppermute | solution.py:18
  440.8 36.1 %collective-permute-start.5 = (bf16[256,16,1]{0,2,1:T(2,128)(2,1)S(1)}, bf16[256,16,1]{0,2,1:T(2,128)(2,1)S(1)}, u32[]{:S(2)}, u32[]{:S(2)}) collective-permute-start(bf16[256,16,1]{0,2,1:T(2,128)(2,1)S(1)} %get-tuple-element.1002), channel_id=1, source_target_pairs={{0,1},{1,2},{2,3},{3,4},{4,5},{5,6},{6,7},{7,8},{8,9},{9,10},{10,1... | collective-permute-start | bytes 24584 | tf_op jit(solution)/shard_map/while/body/eval_jaxpr/ppermute | solution.py:18
  484.9 42.0 %collective-permute-start.2 = (bf16[256,1,16]{0,2,1:T(8,128)(2,1)S(1)}, bf16[256,1,16]{0,2,1:T(8,128)(2,1)S(1)}, u32[]{:S(2)}, u32[]{:S(2)}) collective-permute-start(bf16[256,1,16]{0,2,1:T(8,128)(2,1)S(1)} %get-tuple-element.999), channel_id=1, source_target_pairs={{8,0},{9,1},{10,2},{11,3},{12,4},{13,5},{14,6},{15,7},{16,8},{17,9... | collective-permute-start | bytes 24584 | tf_op jit(solution)/shard_map/while/body/eval_jaxpr/ppermute | solution.py:18
  488.8 38.0 %collective-permute-start.4 = (bf16[256,16,1]{0,2,1:T(2,128)(2,1)S(1)}, bf16[256,16,1]{0,2,1:T(2,128)(2,1)S(1)}, u32[]{:S(2)}, u32[]{:S(2)}) collective-permute-start(bf16[256,16,1]{0,2,1:T(2,128)(2,1)S(1)} %get-tuple-element.1001), channel_id=1, source_target_pairs={{1,0},{2,1},{3,2},{4,3},{5,4},{6,5},{7,6},{8,7},{9,8},{10,9},{11,1... | collective-permute-start | bytes 24584 | tf_op jit(solution)/shard_map/while/body/eval_jaxpr/ppermute | solution.py:18
  490.7 36.1 %collective-permute-start.5 = (bf16[256,16,1]{0,2,1:T(2,128)(2,1)S(1)}, bf16[256,16,1]{0,2,1:T(2,128)(2,1)S(1)}, u32[]{:S(2)}, u32[]{:S(2)}) collective-permute-start(bf16[256,16,1]{0,2,1:T(2,128)(2,1)S(1)} %get-tuple-element.1002), channel_id=1, source_target_pairs={{0,1},{1,2},{2,3},{3,4},{4,5},{5,6},{6,7},{7,8},{8,9},{9,10},{10,1... | collective-permute-start | bytes 24584 | tf_op jit(solution)/shard_map/while/body/eval_jaxpr/ppermute | solution.py:18
  534.7 42.0 %collective-permute-start.2 = (bf16[256,1,16]{0,2,1:T(8,128)(2,1)S(1)}, bf16[256,1,16]{0,2,1:T(8,128)(2,1)S(1)}, u32[]{:S(2)}, u32[]{:S(2)}) collective-permute-start(bf16[256,1,16]{0,2,1:T(8,128)(2,1)S(1)} %get-tuple-element.999), channel_id=1, source_target_pairs={{8,0},{9,1},{10,2},{11,3},{12,4},{13,5},{14,6},{15,7},{16,8},{17,9... | collective-permute-start | bytes 24584 | tf_op jit(solution)/shard_map/while/body/eval_jaxpr/ppermute | solution.py:18
  538.6 38.0 %collective-permute-start.4 = (bf16[256,16,1]{0,2,1:T(2,128)(2,1)S(1)}, bf16[256,16,1]{0,2,1:T(2,128)(2,1)S(1)}, u32[]{:S(2)}, u32[]{:S(2)}) collective-permute-start(bf16[256,16,1]{0,2,1:T(2,128)(2,1)S(1)} %get-tuple-element.1001), channel_id=1, source_target_pairs={{1,0},{2,1},{3,2},{4,3},{5,4},{6,5},{7,6},{8,7},{9,8},{10,9},{11,1... | collective-permute-start | bytes 24584 | tf_op jit(solution)/shard_map/while/body/eval_jaxpr/ppermute | solution.py:18
  591.4 42.2 %collective-permute-start.11 = (bf16[512,1,16]{0,2,1:T(8,128)(2,1)S(1)}, bf16[512,1,16]{0,2,1:T(8,128)(2,1)S(1)}, u32[]{:S(2)}, u32[]{:S(2)}) collective-permute-start(bf16[512,1,16]{0,2,1:T(8,128)(2,1)S(1)} %get-tuple-element.1029), channel_id=1, source_target_pairs={{8,0},{9,1},{10,2},{11,3},{12,4},{13,5},{14,6},{15,7},{16,8},{17,9... | collective-permute-start | bytes 49160 | tf_op jit(solution)/shard_map/while/body/eval_jaxpr/ppermute | solution.py:18
  595.3 38.0 %collective-permute-start.13 = (bf16[512,16,1]{0,2,1:T(2,128)(2,1)S(1)}, bf16[512,16,1]{0,2,1:T(2,128)(2,1)S(1)}, u32[]{:S(2)}, u32[]{:S(2)}) collective-permute-start(bf16[512,16,1]{0,2,1:T(2,128)(2,1)S(1)} %get-tuple-element.1031), channel_id=1, source_target_pairs={{1,0},{2,1},{3,2},{4,3},{5,4},{6,5},{7,6},{8,7},{9,8},{10,9},{11,1... | collective-permute-start | bytes 49160 | tf_op jit(solution)/shard_map/while/body/eval_jaxpr/ppermute | solution.py:18
  597.2 36.1 %collective-permute-start.14 = (bf16[512,16,1]{0,2,1:T(2,128)(2,1)S(1)}, bf16[512,16,1]{0,2,1:T(2,128)(2,1)S(1)}, u32[]{:S(2)}, u32[]{:S(2)}) collective-permute-start(bf16[512,16,1]{0,2,1:T(2,128)(2,1)S(1)} %get-tuple-element.1032), channel_id=1, source_target_pairs={{0,1},{1,2},{2,3},{3,4},{4,5},{5,6},{6,7},{7,8},{8,9},{9,10},{10,1... | collective-permute-start | bytes 49160 | tf_op jit(solution)/shard_map/while/body/eval_jaxpr/ppermute | solution.py:18
  645.5 42.2 %collective-permute-start.11 = (bf16[512,1,16]{0,2,1:T(8,128)(2,1)S(1)}, bf16[512,1,16]{0,2,1:T(8,128)(2,1)S(1)}, u32[]{:S(2)}, u32[]{:S(2)}) collective-permute-start(bf16[512,1,16]{0,2,1:T(8,128)(2,1)S(1)} %get-tuple-element.1029), channel_id=1, source_target_pairs={{8,0},{9,1},{10,2},{11,3},{12,4},{13,5},{14,6},{15,7},{16,8},{17,9... | collective-permute-start | bytes 49160 | tf_op jit(solution)/shard_map/while/body/eval_jaxpr/ppermute | solution.py:18
  649.3 38.0 %collective-permute-start.13 = (bf16[512,16,1]{0,2,1:T(2,128)(2,1)S(1)}, bf16[512,16,1]{0,2,1:T(2,128)(2,1)S(1)}, u32[]{:S(2)}, u32[]{:S(2)}) collective-permute-start(bf16[512,16,1]{0,2,1:T(2,128)(2,1)S(1)} %get-tuple-element.1031), channel_id=1, source_target_pairs={{1,0},{2,1},{3,2},{4,3},{5,4},{6,5},{7,6},{8,7},{9,8},{10,9},{11,1... | collective-permute-start | bytes 49160 | tf_op jit(solution)/shard_map/while/body/eval_jaxpr/ppermute | solution.py:18
  651.3 36.1 %collective-permute-start.14 = (bf16[512,16,1]{0,2,1:T(2,128)(2,1)S(1)}, bf16[512,16,1]{0,2,1:T(2,128)(2,1)S(1)}, u32[]{:S(2)}, u32[]{:S(2)}) collective-permute-start(bf16[512,16,1]{0,2,1:T(2,128)(2,1)S(1)} %get-tuple-element.1032), channel_id=1, source_target_pairs={{0,1},{1,2},{2,3},{3,4},{4,5},{5,6},{6,7},{7,8},{8,9},{9,10},{10,1... | collective-permute-start | bytes 49160 | tf_op jit(solution)/shard_map/while/body/eval_jaxpr/ppermute | solution.py:18
  697.2 42.2 %collective-permute-start.11 = (bf16[512,1,16]{0,2,1:T(8,128)(2,1)S(1)}, bf16[512,1,16]{0,2,1:T(8,128)(2,1)S(1)}, u32[]{:S(2)}, u32[]{:S(2)}) collective-permute-start(bf16[512,1,16]{0,2,1:T(8,128)(2,1)S(1)} %get-tuple-element.1029), channel_id=1, source_target_pairs={{8,0},{9,1},{10,2},{11,3},{12,4},{13,5},{14,6},{15,7},{16,8},{17,9... | collective-permute-start | bytes 49160 | tf_op jit(solution)/shard_map/while/body/eval_jaxpr/ppermute | solution.py:18
  701.1 38.0 %collective-permute-start.13 = (bf16[512,16,1]{0,2,1:T(2,128)(2,1)S(1)}, bf16[512,16,1]{0,2,1:T(2,128)(2,1)S(1)}, u32[]{:S(2)}, u32[]{:S(2)}) collective-permute-start(bf16[512,16,1]{0,2,1:T(2,128)(2,1)S(1)} %get-tuple-element.1031), channel_id=1, source_target_pairs={{1,0},{2,1},{3,2},{4,3},{5,4},{6,5},{7,6},{8,7},{9,8},{10,9},{11,1... | collective-permute-start | bytes 49160 | tf_op jit(solution)/shard_map/while/body/eval_jaxpr/ppermute | solution.py:18
  703.0 36.1 %collective-permute-start.14 = (bf16[512,16,1]{0,2,1:T(2,128)(2,1)S(1)}, bf16[512,16,1]{0,2,1:T(2,128)(2,1)S(1)}, u32[]{:S(2)}, u32[]{:S(2)}) collective-permute-start(bf16[512,16,1]{0,2,1:T(2,128)(2,1)S(1)} %get-tuple-element.1032), channel_id=1, source_target_pairs={{0,1},{1,2},{2,3},{3,4},{4,5},{5,6},{6,7},{7,8},{8,9},{9,10},{10,1... | collective-permute-start | bytes 49160 | tf_op jit(solution)/shard_map/while/body/eval_jaxpr/ppermute | solution.py:18
  749.1 42.2 %collective-permute-start.11 = (bf16[512,1,16]{0,2,1:T(8,128)(2,1)S(1)}, bf16[512,1,16]{0,2,1:T(8,128)(2,1)S(1)}, u32[]{:S(2)}, u32[]{:S(2)}) collective-permute-start(bf16[512,1,16]{0,2,1:T(8,128)(2,1)S(1)} %get-tuple-element.1029), channel_id=1, source_target_pairs={{8,0},{9,1},{10,2},{11,3},{12,4},{13,5},{14,6},{15,7},{16,8},{17,9... | collective-permute-start | bytes 49160 | tf_op jit(solution)/shard_map/while/body/eval_jaxpr/ppermute | solution.py:18
  753.0 38.0 %collective-permute-start.13 = (bf16[512,16,1]{0,2,1:T(2,128)(2,1)S(1)}, bf16[512,16,1]{0,2,1:T(2,128)(2,1)S(1)}, u32[]{:S(2)}, u32[]{:S(2)}) collective-permute-start(bf16[512,16,1]{0,2,1:T(2,128)(2,1)S(1)} %get-tuple-element.1031), channel_id=1, source_target_pairs={{1,0},{2,1},{3,2},{4,3},{5,4},{6,5},{7,6},{8,7},{9,8},{10,9},{11,1... | collective-permute-start | bytes 49160 | tf_op jit(solution)/shard_map/while/body/eval_jaxpr/ppermute | solution.py:18
  754.9 36.1 %collective-permute-start.14 = (bf16[512,16,1]{0,2,1:T(2,128)(2,1)S(1)}, bf16[512,16,1]{0,2,1:T(2,128)(2,1)S(1)}, u32[]{:S(2)}, u32[]{:S(2)}) collective-permute-start(bf16[512,16,1]{0,2,1:T(2,128)(2,1)S(1)} %get-tuple-element.1032), channel_id=1, source_target_pairs={{0,1},{1,2},{2,3},{3,4},{4,5},{5,6},{6,7},{7,8},{8,9},{9,10},{10,1... | collective-permute-start | bytes 49160 | tf_op jit(solution)/shard_map/while/body/eval_jaxpr/ppermute | solution.py:18
  800.9 42.2 %collective-permute-start.11 = (bf16[512,1,16]{0,2,1:T(8,128)(2,1)S(1)}, bf16[512,1,16]{0,2,1:T(8,128)(2,1)S(1)}, u32[]{:S(2)}, u32[]{:S(2)}) collective-permute-start(bf16[512,1,16]{0,2,1:T(8,128)(2,1)S(1)} %get-tuple-element.1029), channel_id=1, source_target_pairs={{8,0},{9,1},{10,2},{11,3},{12,4},{13,5},{14,6},{15,7},{16,8},{17,9... | collective-permute-start | bytes 49160 | tf_op jit(solution)/shard_map/while/body/eval_jaxpr/ppermute | solution.py:18
  804.8 38.0 %collective-permute-start.13 = (bf16[512,16,1]{0,2,1:T(2,128)(2,1)S(1)}, bf16[512,16,1]{0,2,1:T(2,128)(2,1)S(1)}, u32[]{:S(2)}, u32[]{:S(2)}) collective-permute-start(bf16[512,16,1]{0,2,1:T(2,128)(2,1)S(1)} %get-tuple-element.1031), channel_id=1, source_target_pairs={{1,0},{2,1},{3,2},{4,3},{5,4},{6,5},{7,6},{8,7},{9,8},{10,9},{11,1... | collective-permute-start | bytes 49160 | tf_op jit(solution)/shard_map/while/body/eval_jaxpr/ppermute | solution.py:18
  806.7 36.1 %collective-permute-start.14 = (bf16[512,16,1]{0,2,1:T(2,128)(2,1)S(1)}, bf16[512,16,1]{0,2,1:T(2,128)(2,1)S(1)}, u32[]{:S(2)}, u32[]{:S(2)}) collective-permute-start(bf16[512,16,1]{0,2,1:T(2,128)(2,1)S(1)} %get-tuple-element.1032), channel_id=1, source_target_pairs={{0,1},{1,2},{2,3},{3,4},{4,5},{5,6},{6,7},{7,8},{8,9},{9,10},{10,1... | collective-permute-start | bytes 49160 | tf_op jit(solution)/shard_map/while/body/eval_jaxpr/ppermute | solution.py:18
  852.8 42.2 %collective-permute-start.11 = (bf16[512,1,16]{0,2,1:T(8,128)(2,1)S(1)}, bf16[512,1,16]{0,2,1:T(8,128)(2,1)S(1)}, u32[]{:S(2)}, u32[]{:S(2)}) collective-permute-start(bf16[512,1,16]{0,2,1:T(8,128)(2,1)S(1)} %get-tuple-element.1029), channel_id=1, source_target_pairs={{8,0},{9,1},{10,2},{11,3},{12,4},{13,5},{14,6},{15,7},{16,8},{17,9... | collective-permute-start | bytes 49160 | tf_op jit(solution)/shard_map/while/body/eval_jaxpr/ppermute | solution.py:18
  856.7 38.0 %collective-permute-start.13 = (bf16[512,16,1]{0,2,1:T(2,128)(2,1)S(1)}, bf16[512,16,1]{0,2,1:T(2,128)(2,1)S(1)}, u32[]{:S(2)}, u32[]{:S(2)}) collective-permute-start(bf16[512,16,1]{0,2,1:T(2,128)(2,1)S(1)} %get-tuple-element.1031), channel_id=1, source_target_pairs={{1,0},{2,1},{3,2},{4,3},{5,4},{6,5},{7,6},{8,7},{9,8},{10,9},{11,1... | collective-permute-start | bytes 49160 | tf_op jit(solution)/shard_map/while/body/eval_jaxpr/ppermute | solution.py:18
  858.6 36.1 %collective-permute-start.14 = (bf16[512,16,1]{0,2,1:T(2,128)(2,1)S(1)}, bf16[512,16,1]{0,2,1:T(2,128)(2,1)S(1)}, u32[]{:S(2)}, u32[]{:S(2)}) collective-permute-start(bf16[512,16,1]{0,2,1:T(2,128)(2,1)S(1)} %get-tuple-element.1032), channel_id=1, source_target_pairs={{0,1},{1,2},{2,3},{3,4},{4,5},{5,6},{6,7},{7,8},{8,9},{9,10},{10,1... | collective-permute-start | bytes 49160 | tf_op jit(solution)/shard_map/while/body/eval_jaxpr/ppermute | solution.py:18
  904.6 42.2 %collective-permute-start.11 = (bf16[512,1,16]{0,2,1:T(8,128)(2,1)S(1)}, bf16[512,1,16]{0,2,1:T(8,128)(2,1)S(1)}, u32[]{:S(2)}, u32[]{:S(2)}) collective-permute-start(bf16[512,1,16]{0,2,1:T(8,128)(2,1)S(1)} %get-tuple-element.1029), channel_id=1, source_target_pairs={{8,0},{9,1},{10,2},{11,3},{12,4},{13,5},{14,6},{15,7},{16,8},{17,9... | collective-permute-start | bytes 49160 | tf_op jit(solution)/shard_map/while/body/eval_jaxpr/ppermute | solution.py:18
  908.4 38.0 %collective-permute-start.13 = (bf16[512,16,1]{0,2,1:T(2,128)(2,1)S(1)}, bf16[512,16,1]{0,2,1:T(2,128)(2,1)S(1)}, u32[]{:S(2)}, u32[]{:S(2)}) collective-permute-start(bf16[512,16,1]{0,2,1:T(2,128)(2,1)S(1)} %get-tuple-element.1031), channel_id=1, source_target_pairs={{1,0},{2,1},{3,2},{4,3},{5,4},{6,5},{7,6},{8,7},{9,8},{10,9},{11,1... | collective-permute-start | bytes 49160 | tf_op jit(solution)/shard_map/while/body/eval_jaxpr/ppermute | solution.py:18
  910.4 36.1 %collective-permute-start.14 = (bf16[512,16,1]{0,2,1:T(2,128)(2,1)S(1)}, bf16[512,16,1]{0,2,1:T(2,128)(2,1)S(1)}, u32[]{:S(2)}, u32[]{:S(2)}) collective-permute-start(bf16[512,16,1]{0,2,1:T(2,128)(2,1)S(1)} %get-tuple-element.1032), channel_id=1, source_target_pairs={{0,1},{1,2},{2,3},{3,4},{4,5},{5,6},{6,7},{7,8},{8,9},{9,10},{10,1... | collective-permute-start | bytes 49160 | tf_op jit(solution)/shard_map/while/body/eval_jaxpr/ppermute | solution.py:18
  986.0 42.2 %collective-permute-start.11 = (bf16[512,1,16]{0,2,1:T(8,128)(2,1)S(1)}, bf16[512,1,16]{0,2,1:T(8,128)(2,1)S(1)}, u32[]{:S(2)}, u32[]{:S(2)}) collective-permute-start(bf16[512,1,16]{0,2,1:T(8,128)(2,1)S(1)} %get-tuple-element.1029), channel_id=1, source_target_pairs={{8,0},{9,1},{10,2},{11,3},{12,4},{13,5},{14,6},{15,7},{16,8},{17,9... | collective-permute-start | bytes 49160 | tf_op jit(solution)/shard_map/while/body/eval_jaxpr/ppermute | solution.py:18
  989.8 38.0 %collective-permute-start.13 = (bf16[512,16,1]{0,2,1:T(2,128)(2,1)S(1)}, bf16[512,16,1]{0,2,1:T(2,128)(2,1)S(1)}, u32[]{:S(2)}, u32[]{:S(2)}) collective-permute-start(bf16[512,16,1]{0,2,1:T(2,128)(2,1)S(1)} %get-tuple-element.1031), channel_id=1, source_target_pairs={{1,0},{2,1},{3,2},{4,3},{5,4},{6,5},{7,6},{8,7},{9,8},{10,9},{11,1... | collective-permute-start | bytes 49160 | tf_op jit(solution)/shard_map/while/body/eval_jaxpr/ppermute | solution.py:18
  991.8 36.1 %collective-permute-start.14 = (bf16[512,16,1]{0,2,1:T(2,128)(2,1)S(1)}, bf16[512,16,1]{0,2,1:T(2,128)(2,1)S(1)}, u32[]{:S(2)}, u32[]{:S(2)}) collective-permute-start(bf16[512,16,1]{0,2,1:T(2,128)(2,1)S(1)} %get-tuple-element.1032), channel_id=1, source_target_pairs={{0,1},{1,2},{2,3},{3,4},{4,5},{5,6},{6,7},{7,8},{8,9},{9,10},{10,1... | collective-permute-start | bytes 49160 | tf_op jit(solution)/shard_map/while/body/eval_jaxpr/ppermute | solution.py:18
  1042.7 42.2 %collective-permute-start.11 = (bf16[512,1,16]{0,2,1:T(8,128)(2,1)S(1)}, bf16[512,1,16]{0,2,1:T(8,128)(2,1)S(1)}, u32[]{:S(2)}, u32[]{:S(2)}) collective-permute-start(bf16[512,1,16]{0,2,1:T(8,128)(2,1)S(1)} %get-tuple-element.1029), channel_id=1, source_target_pairs={{8,0},{9,1},{10,2},{11,3},{12,4},{13,5},{14,6},{15,7},{16,8},{17,9... | collective-permute-start | bytes 49160 | tf_op jit(solution)/shard_map/while/body/eval_jaxpr/ppermute | solution.py:18
  1046.6 38.0 %collective-permute-start.13 = (bf16[512,16,1]{0,2,1:T(2,128)(2,1)S(1)}, bf16[512,16,1]{0,2,1:T(2,128)(2,1)S(1)}, u32[]{:S(2)}, u32[]{:S(2)}) collective-permute-start(bf16[512,16,1]{0,2,1:T(2,128)(2,1)S(1)} %get-tuple-element.1031), channel_id=1, source_target_pairs={{1,0},{2,1},{3,2},{4,3},{5,4},{6,5},{7,6},{8,7},{9,8},{10,9},{11,1... | collective-permute-start | bytes 49160 | tf_op jit(solution)/shard_map/while/body/eval_jaxpr/ppermute | solution.py:18
  1048.5 36.1 %collective-permute-start.14 = (bf16[512,16,1]{0,2,1:T(2,128)(2,1)S(1)}, bf16[512,16,1]{0,2,1:T(2,128)(2,1)S(1)}, u32[]{:S(2)}, u32[]{:S(2)}) collective-permute-start(bf16[512,16,1]{0,2,1:T(2,128)(2,1)S(1)} %get-tuple-element.1032), channel_id=1, source_target_pairs={{0,1},{1,2},{2,3},{3,4},{4,5},{5,6},{6,7},{7,8},{8,9},{9,10},{10,1... | collective-permute-start | bytes 49160 | tf_op jit(solution)/shard_map/while/body/eval_jaxpr/ppermute | solution.py:18
  1099.4 42.2 %collective-permute-start.11 = (bf16[512,1,16]{0,2,1:T(8,128)(2,1)S(1)}, bf16[512,1,16]{0,2,1:T(8,128)(2,1)S(1)}, u32[]{:S(2)}, u32[]{:S(2)}) collective-permute-start(bf16[512,1,16]{0,2,1:T(8,128)(2,1)S(1)} %get-tuple-element.1029), channel_id=1, source_target_pairs={{8,0},{9,1},{10,2},{11,3},{12,4},{13,5},{14,6},{15,7},{16,8},{17,9... | collective-permute-start | bytes 49160 | tf_op jit(solution)/shard_map/while/body/eval_jaxpr/ppermute | solution.py:18
  1103.3 38.0 %collective-permute-start.13 = (bf16[512,16,1]{0,2,1:T(2,128)(2,1)S(1)}, bf16[512,16,1]{0,2,1:T(2,128)(2,1)S(1)}, u32[]{:S(2)}, u32[]{:S(2)}) collective-permute-start(bf16[512,16,1]{0,2,1:T(2,128)(2,1)S(1)} %get-tuple-element.1031), channel_id=1, source_target_pairs={{1,0},{2,1},{3,2},{4,3},{5,4},{6,5},{7,6},{8,7},{9,8},{10,9},{11,1... | collective-permute-start | bytes 49160 | tf_op jit(solution)/shard_map/while/body/eval_jaxpr/ppermute | solution.py:18
  1105.2 36.1 %collective-permute-start.14 = (bf16[512,16,1]{0,2,1:T(2,128)(2,1)S(1)}, bf16[512,16,1]{0,2,1:T(2,128)(2,1)S(1)}, u32[]{:S(2)}, u32[]{:S(2)}) collective-permute-start(bf16[512,16,1]{0,2,1:T(2,128)(2,1)S(1)} %get-tuple-element.1032), channel_id=1, source_target_pairs={{0,1},{1,2},{2,3},{3,4},{4,5},{5,6},{6,7},{7,8},{8,9},{9,10},{10,1... | collective-permute-start | bytes 49160 | tf_op jit(solution)/shard_map/while/body/eval_jaxpr/ppermute | solution.py:18
  1156.1 42.2 %collective-permute-start.11 = (bf16[512,1,16]{0,2,1:T(8,128)(2,1)S(1)}, bf16[512,1,16]{0,2,1:T(8,128)(2,1)S(1)}, u32[]{:S(2)}, u32[]{:S(2)}) collective-permute-start(bf16[512,1,16]{0,2,1:T(8,128)(2,1)S(1)} %get-tuple-element.1029), channel_id=1, source_target_pairs={{8,0},{9,1},{10,2},{11,3},{12,4},{13,5},{14,6},{15,7},{16,8},{17,9... | collective-permute-start | bytes 49160 | tf_op jit(solution)/shard_map/while/body/eval_jaxpr/ppermute | solution.py:18
  1160.0 38.0 %collective-permute-start.13 = (bf16[512,16,1]{0,2,1:T(2,128)(2,1)S(1)}, bf16[512,16,1]{0,2,1:T(2,128)(2,1)S(1)}, u32[]{:S(2)}, u32[]{:S(2)}) collective-permute-start(bf16[512,16,1]{0,2,1:T(2,128)(2,1)S(1)} %get-tuple-element.1031), channel_id=1, source_target_pairs={{1,0},{2,1},{3,2},{4,3},{5,4},{6,5},{7,6},{8,7},{9,8},{10,9},{11,1... | collective-permute-start | bytes 49160 | tf_op jit(solution)/shard_map/while/body/eval_jaxpr/ppermute | solution.py:18
  1161.9 36.1 %collective-permute-start.14 = (bf16[512,16,1]{0,2,1:T(2,128)(2,1)S(1)}, bf16[512,16,1]{0,2,1:T(2,128)(2,1)S(1)}, u32[]{:S(2)}, u32[]{:S(2)}) collective-permute-start(bf16[512,16,1]{0,2,1:T(2,128)(2,1)S(1)} %get-tuple-element.1032), channel_id=1, source_target_pairs={{0,1},{1,2},{2,3},{3,4},{4,5},{5,6},{6,7},{7,8},{8,9},{9,10},{10,1... | collective-permute-start | bytes 49160 | tf_op jit(solution)/shard_map/while/body/eval_jaxpr/ppermute | solution.py:18
  (136 other events, 2069.5 us)
where the time goes:
time: 1210 us; the launch traced here: 1200 us
  starting transfers between devices  834 us (69%)
  waiting for transfers between devices  269 us (22%)
  other arithmetic  58.8 us (5%)
  local copies, waits for them, and re-layouts  18 us (1%)
  matrix products  17.6 us (1%)
    ppermute x198, starting transfers between devices, from_behind(): lax.ppermute(value, axis, [(source, source + steps) for source in range(i...  834 us
    ppermute x198, waiting for transfers between devices, from_behind(): lax.ppermute(value, axis, [(source, source + steps) for source in range(i...  269 us
    another operation x22, other arithmetic  33.6 us
  transfers between devices with their start and end apart: 198, of which 87 were waited for; matrix products, arithmetic and copies ran while one was open for 1% of the time, Pallas kernels for 0%

commit v1 on v0

v1 whole, which is shorter than its diff:
```python
import jax
import jax.numpy as jnp
from jax import lax
from jax.experimental import pallas as pl
from jax.experimental.pallas import tpu as pltpu
from jax.sharding import PartitionSpec as P

TG = 8
TR = 16
TC = 16
CH = 128
STEPS = 4
PIX = TR * TC
EXT = (TR + 2) * TC
SLOTS = TR + 8
MESH = pl.DeviceIdType.MESH
BF = jnp.bfloat16
F32 = jnp.float32

SLOT_OF = {
    (-1, 0): 0,
    (1, 0): 17,
    (0, -1): 18,
    (0, 1): 19,
    (-1, -1): 20,
    (-1, 1): 21,
    (1, -1): 22,
    (1, 1): 23,
}


def kernel(
    sections,
    tiles,
    frames_ref,
    weights_ref,
    bias_ref,
    cot_ref,
    hidden_ref,
    grads_ref,
    xin,
    hin,
    dzin,
    din,
    hcol,
    dzcol,
    dsend,
    fcol,
    wf,
    wb,
    pick,
    edge,
    win_f,
    win_b,
    gates,
    cells,
    cot_t,
    x_sem,
    h_sem,
    dz_sem,
    d_sem,
    xs_sem,
    hs_sem,
    dzs_sem,
    ds_sem,
    w_sem,
):
    sec = lax.axis_index("section")
    tile = lax.axis_index("tile")
    grid_rows = tiles // TG
    row = lax.div(tile, TG)
    col = lax.rem(tile, TG)
    first = sec == 0
    last = sec == sections - 1

    def at(delta_row, delta_col):
        there_row = lax.rem(row + (delta_row + grid_rows), grid_rows)
        there_col = lax.rem(col + (delta_col + TG), TG)
        return there_row * TG + there_col

    copies = []
    for a in range(3):
        for b in range(3):
            copies.append(
                pltpu.make_async_copy(
                    weights_ref.at[3 * a + b], wf.at[a, :, pl.ds(2 * CH * b, 2 * CH)], w_sem.at[0, 3 * a + b]
                )
            )
            copies.append(
                pltpu.make_async_copy(
                    weights_ref.at[3 * a + 2 - b], wb.at[a, pl.ds(4 * CH * b, 4 * CH), :], w_sem.at[1, 3 * a + b]
                )
            )
    for copy in copies:
        copy.start()

    barrier = pltpu.get_barrier_semaphore()
    for delta in SLOT_OF:
        pl.semaphore_signal(barrier, inc=1, device_id={"section": sec, "tile": at(*delta)}, device_id_type=MESH)

    @pl.when(sec > 0)
    def _():
        for delta in SLOT_OF:
            pl.semaphore_signal(
                barrier, inc=1, device_id={"section": sec - 1, "tile": at(*delta)}, device_id_type=MESH
            )
        pl.semaphore_signal(barrier, inc=1, device_id={"section": sec - 1, "tile": tile}, device_id_type=MESH)

    @pl.when(sec < sections - 1)
    def _():
        pl.semaphore_signal(barrier, inc=1, device_id={"section": sec + 1, "tile": tile}, device_id_type=MESH)

    up_ok = row > 0
    down_ok = row < grid_rows - 1
    left_ok = col > 0
    right_ok = col < TG - 1
    out_at = lax.broadcasted_iota(jnp.int32, (EXT, SLOTS * TC), 0)
    src_at = lax.broadcasted_iota(jnp.int32, (EXT, SLOTS * TC), 1)
    r_at = lax.shift_right_logical(out_at, 4)
    q_at = lax.bitwise_and(out_at, TC - 1)
    bad_row = ((r_at == 0) & jnp.logical_not(up_ok)) | ((r_at == TR + 1) & jnp.logical_not(down_ok))
    for side in range(2):
        rim_q = 0 if side == 0 else TC - 1
        step = -1 if side == 0 else 1
        far = TC - 1 if side == 0 else 0
        side_ok = left_ok if side == 0 else right_ok
        rim_src = jnp.where(
            r_at == 0,
            (20 + side) * TC + far,
            jnp.where(r_at == TR + 1, (22 + side) * TC + far, (18 + side) * TC + r_at - 1),
        )
        on_rim = q_at == rim_q
        source = jnp.where(on_rim, rim_src, out_at + step)
        bad = bad_row | (on_rim & jnp.logical_not(side_ok))
        source = jnp.where(bad, -1, source)
        pick[side] = jnp.where(src_at == source, 1.0, 0.0).astype(BF)
    edge_out = lax.broadcasted_iota(jnp.int32, (2 * TR, PIX), 0)
    edge_src = lax.broadcasted_iota(jnp.int32, (2 * TR, PIX), 1)
    edge_want = jnp.where(edge_out < TR, edge_out * TC, (edge_out - TR) * TC + TC - 1)
    edge[...] = jnp.where(edge_src == edge_want, 1.0, 0.0).astype(BF)

    def columns(field):
        return jnp.dot(edge[...], field, preferred_element_type=F32).astype(BF)

    def rims(tile_buf, col_buf, dst, dst_t, section, send_sem, recv_sem):
        out = []
        for (delta_row, delta_col), slot in SLOT_OF.items():
            if delta_row == -1:
                piece = tile_buf.at[TR]
            elif delta_row == 1:
                piece = tile_buf.at[1]
            elif delta_col == -1:
                piece = col_buf.at[1]
            else:
                piece = col_buf.at[0]
            out.append(
                pltpu.make_async_remote_copy(
                    src_ref=piece,
                    dst_ref=dst.at[dst_t, slot],
                    send_sem=send_sem,
                    recv_sem=recv_sem,
                    device_id={"section": section, "tile": at(-delta_row, -delta_col)},
                    device_id_type=MESH,
                )
            )
        return out

    def wait_for(buf, sem):
        pltpu.make_async_copy(buf, buf, sem).wait()

    def turn_cotangent():
        def turn(t, carry):
            cot_t[t] = cot_ref[t].astype(F32).T
            return carry

        lax.fori_loop(0, STEPS, turn, 0)

    hin[0] = jnp.zeros((SLOTS, TC, CH), BF)

    @pl.when(first)
    def _():
        def place(t, carry):
            field = frames_ref[t].astype(F32).T.astype(BF)
            xin[t, 1 : TR + 1] = field.reshape(TR, TC, CH)
            fcol[t] = columns(field).reshape(2, TR, CH)
            return carry

        lax.fori_loop(0, STEPS, place, 0)

    @pl.when(sec > 0)
    def _():
        turn_cotangent()

    pl.semaphore_wait(
        barrier,
        8 + jnp.where(last, 0, 9) + jnp.where(first, 0, 1),
    )

    @pl.when(first)
    def _():
        def share(t, carry):
            for copy in rims(xin.at[t], fcol.at[t], xin, t, sec, xs_sem.at[t], x_sem.at[t]):
                copy.start()
            return carry

        lax.fori_loop(0, STEPS, share, 0)

    for copy in copies[0::2]:
        copy.wait()

    up_f = jnp.where(up_ok, 1.0, 0.0)
    down_f = jnp.where(down_ok, 1.0, 0.0)

    def middle(buf, t, width):
        top = (buf[t, 0].astype(F32) * up_f).astype(BF)
        low = (buf[t, TR + 1].astype(F32) * down_f).astype(BF)
        return top, buf[t, 1 : TR + 1].reshape(PIX, width), low

    def spread(buf, t, width, win, base, stride):
        whole = buf[t].reshape(SLOTS * TC, width)
        for side in range(2):
            moved = jnp.dot(pick[side], whole, preferred_element_type=F32).astype(BF)
            win[:, pl.ds(2 * side * stride + base, width)] = moved
        top, mid, low = middle(buf, t, width)
        win[0:TC, pl.ds(stride + base, width)] = top
        win[TC : TC + PIX, pl.ds(stride + base, width)] = mid
        win[TC + PIX : EXT, pl.ds(stride + base, width)] = low

    cells[0] = jnp.zeros((PIX, CH), F32)

    def forward(t, carry):
        @pl.when(t > 0)
        def _():
            wait_for(hin.at[t, pl.ds(0, 8)], h_sem.at[t])

        spread(hin, t, CH, win_f, CH, 2 * CH)

        @pl.when(first)
        def _():
            wait_for(xin.at[t, pl.ds(0, 8)], x_sem.at[t])

        @pl.when(sec > 0)
        def _():
            wait_for(xin.at[t], x_sem.at[t])

        spread(xin, t, CH, win_f, 0, 2 * CH)
        z = bias_ref[...]
        for a in range(3):
            z = z + lax.dot_general(
                win_f[a * TC : a * TC + PIX, :],
                wf[a],
                (((1,), (1,)), ((), ())),
                preferred_element_type=F32,
            )
        in_gate = jax.nn.sigmoid(z[:, :CH])
        forget = jax.nn.sigmoid(z[:, CH : 2 * CH])
        cand = jnp.tanh(z[:, 2 * CH : 3 * CH])
        out_gate = jax.nn.sigmoid(z[:, 3 * CH :])
        cell = forget * cells[t] + in_gate * cand
        hidden = out_gate * jnp.tanh(cell)
        field = hidden.astype(BF)
        hin[t + 1, 1 : TR + 1] = field.reshape(TR, TC, CH)
        hcol[t] = columns(field).reshape(2, TR, CH)

        @pl.when(sec < sections - 1)
        def _():
            pltpu.make_async_remote_copy(
                src_ref=hin.at[t + 1, pl.ds(1, TR)],
                dst_ref=xin.at[t, pl.ds(1, TR)],
                send_sem=xs_sem.at[STEPS + t],
                recv_sem=x_sem.at[t],
                device_id={"section": sec + 1, "tile": tile},
                device_id_type=MESH,
            ).start()
            for copy in rims(hin.at[t + 1], hcol.at[t], xin, t, sec + 1, xs_sem.at[STEPS + t], x_sem.at[t]):
                copy.start()

        @pl.when(t < STEPS - 1)
        def _():
            for copy in rims(hin.at[t + 1], hcol.at[t], hin, t + 1, sec, hs_sem.at[t], h_sem.at[t + 1]):
                copy.start()

        gates[t, :, 0:CH] = in_gate
        gates[t, :, CH : 2 * CH] = forget
        gates[t, :, 2 * CH : 3 * CH] = cand
        gates[t, :, 3 * CH :] = out_gate
        cells[t + 1] = cell
        hidden_ref[t] = hidden.T.astype(BF)
        return carry

    lax.fori_loop(0, STEPS, forward, 0)

    @pl.when(first)
    def _():
        turn_cotangent()

    for copy in copies[1::2]:
        copy.wait()

    def backward(back, carry):
        d_rec, d_cell = carry
        t = STEPS - 1 - back

        @pl.when(sec < sections - 1)
        def _():
            wait_for(din.at[t], d_sem.at[t])

        in_gate = gates[t, :, 0:CH]
        forget = gates[t, :, CH : 2 * CH]
        cand = gates[t, :, 2 * CH : 3 * CH]
        out_gate = gates[t, :, 3 * CH :]
        tanh_cell = jnp.tanh(cells[t + 1])
        d_hidden = cot_t[t] + din[t].astype(F32) + d_rec
        d_total = d_cell + d_hidden * out_gate * (1.0 - tanh_cell * tanh_cell)
        parts = [
            d_total * cand * in_gate * (1.0 - in_gate),
            d_total * cells[t] * forget * (1.0 - forget),
            d_total * in_gate * (1.0 - cand * cand),
            d_hidden * tanh_cell * out_gate * (1.0 - out_gate),
        ]
        dz = jnp.concatenate([part.astype(BF) for part in parts], 1)
        dzin[t, 1 : TR + 1] = dz.reshape(TR, TC, 4 * CH)
        dzcol[t] = columns(dz).reshape(2, TR, 4 * CH)
        for copy in rims(dzin.at[t], dzcol.at[t], dzin, t, sec, dzs_sem.at[t], dz_sem.at[t]):
            copy.start()
        wait_for(dzin.at[t, pl.ds(0, 8)], dz_sem.at[t])
        spread(dzin, t, 4 * CH, win_b, 0, 4 * CH)
        du = None
        for a in range(3):
            term = jnp.dot(
                win_b[(2 - a) * TC : (2 - a) * TC + PIX, :], wb[a], preferred_element_type=F32
            )
            du = term if du is None else du + term
        d_input = du[:, :CH]
        dsend[t] = d_input.astype(BF)

        @pl.when(sec > 0)
        def _():
            pltpu.make_async_remote_copy(
                src_ref=dsend.at[t],
                dst_ref=din.at[t],
                send_sem=ds_sem.at[t],
                recv_sem=d_sem.at[t],
                device_id={"section": sec - 1, "tile": tile},
                device_id_type=MESH,
            ).start()

        grads_ref[t] = d_input.T.astype(BF)
        return du[:, CH:], d_total * forget

    @pl.when(last)
    def _():
        din[...] = jnp.zeros(din.shape, BF)

    zero = jnp.zeros((PIX, CH), F32)
    lax.fori_loop(0, STEPS, backward, (zero, zero))

    def settle(t, carry):
        @pl.when(first)
        def _():
            wait_for(xin.at[t, pl.ds(0, 8)], xs_sem.at[t])

        @pl.when(sec < sections - 1)
        def _():
            wait_for(xin.at[t], xs_sem.at[STEPS + t])

        @pl.when(t < STEPS - 1)
        def _():
            wait_for(hin.at[t, pl.ds(0, 8)], hs_sem.at[t])

        wait_for(dzin.at[t, pl.ds(0, 8)], dzs_sem.at[t])

        @pl.when(sec > 0)
        def _():
            wait_for(dsend.at[t], ds_sem.at[t])

        return carry

    lax.fori_loop(0, STEPS, settle, 0)


def make_step(sections, tiles):
    def body(*refs):
        kernel(sections, tiles, *refs)

    return pl.pallas_call(
        body,
        out_shape=[jax.ShapeDtypeStruct((STEPS, CH, PIX), BF)] * 2,
        in_specs=[
            pl.BlockSpec(memory_space=pltpu.VMEM),
            pl.BlockSpec(memory_space=pl.ANY),
            pl.BlockSpec(memory_space=pltpu.VMEM),
            pl.BlockSpec(memory_space=pltpu.VMEM),
        ],
        out_specs=[pl.BlockSpec(memory_space=pltpu.VMEM)] * 2,
        scratch_shapes=[
            pltpu.VMEM((STEPS, SLOTS, TC, CH), BF),
            pltpu.VMEM((STEPS + 1, SLOTS, TC, CH), BF),
            pltpu.VMEM((STEPS, SLOTS, TC, 4 * CH), BF),
            pltpu.VMEM((STEPS, PIX, CH), BF),
            pltpu.VMEM((STEPS, 2, TR, CH), BF),
            pltpu.VMEM((STEPS, 2, TR, 4 * CH), BF),
            pltpu.VMEM((STEPS, PIX, CH), BF),
            pltpu.VMEM((STEPS, 2, TR, CH), BF),
            pltpu.VMEM((3, 4 * CH, 6 * CH), BF),
            pltpu.VMEM((3, 12 * CH, 2 * CH), BF),
            pltpu.VMEM((2, EXT, SLOTS * TC), BF),
            pltpu.VMEM((2 * TR, PIX), BF),
            pltpu.VMEM((EXT, 6 * CH), BF),
            pltpu.VMEM((EXT, 12 * CH), BF),
            pltpu.VMEM((STEPS, PIX, 4 * CH), F32),
            pltpu.VMEM((STEPS + 1, PIX, CH), F32),
            pltpu.VMEM((STEPS, PIX, CH), F32),
            pltpu.SemaphoreType.DMA((STEPS,)),
            pltpu.SemaphoreType.DMA((STEPS,)),
            pltpu.SemaphoreType.DMA((STEPS,)),
            pltpu.SemaphoreType.DMA((STEPS,)),
            pltpu.SemaphoreType.DMA((2 * STEPS,)),
            pltpu.SemaphoreType.DMA((STEPS,)),
            pltpu.SemaphoreType.DMA((STEPS,)),
            pltpu.SemaphoreType.DMA((STEPS,)),
            pltpu.SemaphoreType.DMA((2, 9)),
        ],
        compiler_params=pltpu.CompilerParams(
            collective_id=0, has_side_effects=True, vmem_limit_bytes=56 * 1024 * 1024
        ),
        name="conv_lstm",
    )


def solution(mesh):
    step = make_step(mesh.shape["section"], mesh.shape["tile"])

    def per_device(frames, weights, gate_bias, cotangent):
        hidden, grads = step(
            frames.reshape(STEPS, CH, PIX), weights[0], gate_bias, cotangent.reshape(STEPS, CH, PIX)
        )
        shape = (1, STEPS, CH, 1, PIX)
        return hidden.reshape(shape), grads.reshape(shape)

    in_specs = (
        P(None, None, "tile", None),
        P("section", None, None, None),
        P("section", None),
        P("section", None, None, "tile", None),
    )
    out_specs = (P("section", None, None, "tile", None), P("section", None, None, "tile", None))
    return jax.shard_map(
        per_device, mesh=mesh, in_specs=in_specs, out_specs=out_specs, check_vma=False
    )
```

time: 1210 us -> 214 us (0.18)
  starting transfers between devices: 834 us -> 0 us
  waiting for transfers between devices: 269 us -> 0 us
  Pallas kernels: 0 us -> 210 us
  other arithmetic: 58.8 us -> 0 us
  matrix products: 17.6 us -> 0 us
  local copies, waits for them, and re-layouts: 18 us -> 3.34 us
    ppermute x198 -> x0, starting transfers between devices: 834 us -> none  [from_behind(): lax.ppermute(value, axis, [(source, source + steps) for source in range(i...]
    ppermute x198 -> x0, waiting for transfers between devices: 269 us -> none  [from_behind(): lax.ppermute(value, axis, [(source, source + steps) for source in range(i...]
    pallas_call x0 -> x1, Pallas kernels: none -> 210 us  [per_device(): step(frames.reshape(STEPS, CH, PIX), weights[0], gate_bias, cotangent.res...]
    another operation x22 -> x0, other arithmetic: 33.6 us -> none
    dot_general x72 -> x0, matrix products: 17.6 us -> none  [the longest x36 9.38 us: gate_terms(): jnp.dot(kernel[offset_row * 3 + offset_col], window, preferred_element_ty...]
  transfers between devices with their start and end apart: 198 -> 0, of which waited for: 87 -> 0; matrix products, arithmetic and copies ran while one was open for 1% -> 0% of each run, Pallas kernels for 0% -> 0%
where the time goes in v1:
time: 214 us
  Pallas kernels  210 us (98%)
  local copies, waits for them, and re-layouts  3.34 us (2%)
    pallas_call x1, Pallas kernels, per_device(): step(frames.reshape(STEPS, CH, PIX), weights[0], gate_bias, cotangent.res...  210 us

profile of v1, /device:TPU:6, one launch (start us, length us, event | category | flops | bytes accessed | tf_op | source)
XLA Modules:
  0.0 214.1 jit_solution(3185565772221408838)
XLA Ops:
  0.6 210.1 %conv_lstm.1 = (bf16[4,128,256]{2,1,0:T(8,128)(2,1)}, bf16[4,128,256]{2,1,0:T(8,128)(2,1)}) custom-call(bf16[4,128,256]{2,1,0:T(8,128)(2,1)} %bitcast.10, bf16[9,512,256]{2,1,0:T(8,128)(2,1)} %bitcast.9, f32[1,512]{1,0:T(1,128)} %refs_2_.1, bf16[4,128,256]{2,1,0:T(8,128)(2,1)} %bitcast.11), custom_call_target="tpu_custom_call" | custom-call | tf_op jit(solution)/shard_map/conv_lstm/pallas_call | solution.py:435
  210.8 1.7 copy.10
  212.4 1.7 copy.11

commit v2 on v1

v2 whole, which is shorter than its diff:
```python
import jax
import jax.numpy as jnp
from jax import lax
from jax.experimental import pallas as pl
from jax.experimental.pallas import tpu as pltpu
from jax.sharding import PartitionSpec as P

TG = 8
TR = 16
TC = 16
CH = 128
STEPS = 4
PIX = TR * TC
EXT = (TR + 2) * TC
SLOTS = TR + 8
MESH = pl.DeviceIdType.MESH
BF = jnp.bfloat16
F32 = jnp.float32

NEAR = TR + 2
FAR = 6
FAR_SLOTS = {
    (-1, 0): 18,
    (1, 0): 19,
    (-1, -1): 20,
    (-1, 1): 21,
    (1, -1): 22,
    (1, 1): 23,
}
NEAR_SLOTS = {(0, -1): 16, (0, 1): 17}
SLOT_OF = {**FAR_SLOTS, **NEAR_SLOTS}


def kernel(
    sections,
    tiles,
    frames_ref,
    weights_ref,
    bias_ref,
    cot_ref,
    hidden_ref,
    grads_ref,
    xin,
    hin,
    dzin,
    din,
    hcol,
    dzcol,
    dsend,
    fcol,
    wf,
    wb,
    pick,
    pick_far,
    edge,
    win_f,
    win_b,
    far_f,
    far_b,
    z_ref,
    du_ref,
    dc_ref,
    gates,
    cells,
    cot_t,
    x_sem,
    h_sem,
    dz_sem,
    d_sem,
    xs_sem,
    hs_sem,
    dzs_sem,
    ds_sem,
    w_sem,
):
    sec = lax.axis_index("section")
    tile = lax.axis_index("tile")
    grid_rows = tiles // TG
    row = lax.div(tile, TG)
    col = lax.rem(tile, TG)
    first = sec == 0
    last = sec == sections - 1

    def at(delta_row, delta_col):
        there_row = lax.rem(row + (delta_row + grid_rows), grid_rows)
        there_col = lax.rem(col + (delta_col + TG), TG)
        return there_row * TG + there_col

    copies = []
    for a in range(3):
        for b in range(3):
            copies.append(
                pltpu.make_async_copy(
                    weights_ref.at[3 * a + b], wf.at[a, :, pl.ds(2 * CH * b, 2 * CH)], w_sem.at[0, 3 * a + b]
                )
            )
            copies.append(
                pltpu.make_async_copy(
                    weights_ref.at[3 * a + 2 - b], wb.at[a, pl.ds(4 * CH * b, 4 * CH), :], w_sem.at[1, 3 * a + b]
                )
            )
    for copy in copies:
        copy.start()

    barrier = pltpu.get_barrier_semaphore()
    for delta in SLOT_OF:
        pl.semaphore_signal(barrier, inc=1, device_id={"section": sec, "tile": at(*delta)}, device_id_type=MESH)

    @pl.when(sec > 0)
    def _():
        for delta in SLOT_OF:
            pl.semaphore_signal(
                barrier, inc=1, device_id={"section": sec - 1, "tile": at(*delta)}, device_id_type=MESH
            )
        pl.semaphore_signal(barrier, inc=1, device_id={"section": sec - 1, "tile": tile}, device_id_type=MESH)

    @pl.when(sec < sections - 1)
    def _():
        pl.semaphore_signal(barrier, inc=1, device_id={"section": sec + 1, "tile": tile}, device_id_type=MESH)

    up_ok = row > 0
    down_ok = row < grid_rows - 1
    left_ok = col > 0
    right_ok = col < TG - 1
    out_at = lax.broadcasted_iota(jnp.int32, (PIX, NEAR * TC), 0)
    src_at = lax.broadcasted_iota(jnp.int32, (PIX, NEAR * TC), 1)
    r_at = lax.shift_right_logical(out_at, 4)
    q_at = lax.bitwise_and(out_at, TC - 1)
    for side in range(2):
        side_ok = left_ok if side == 0 else right_ok
        on_rim = q_at == (0 if side == 0 else TC - 1)
        source = jnp.where(on_rim, (TR + side) * TC + r_at, out_at + (2 * side - 1))
        source = jnp.where(on_rim & jnp.logical_not(side_ok), -1, source)
        pick[side] = jnp.where(src_at == source, 1.0, 0.0).astype(BF)
    out_at = lax.broadcasted_iota(jnp.int32, (2 * TC, FAR * TC), 0)
    src_at = lax.broadcasted_iota(jnp.int32, (2 * TC, FAR * TC), 1)
    low = lax.shift_right_logical(out_at, 4)
    q_at = lax.bitwise_and(out_at, TC - 1)
    bad_row = ((low == 0) & jnp.logical_not(up_ok)) | ((low == 1) & jnp.logical_not(down_ok))
    for b in range(3):
        q_src = q_at + (b - 1)
        over_left = q_src < 0
        over_right = q_src >= TC
        source = jnp.where(
            over_left,
            (2 + 2 * low) * TC + TC - 1,
            jnp.where(over_right, (3 + 2 * low) * TC, low * TC + q_src),
        )
        bad = bad_row | (over_left & jnp.logical_not(left_ok)) | (over_right & jnp.logical_not(right_ok))
        source = jnp.where(bad, -1, source)
        pick_far[b] = jnp.where(src_at == source, 1.0, 0.0).astype(BF)
    edge_out = lax.broadcasted_iota(jnp.int32, (2 * TR, PIX), 0)
    edge_src = lax.broadcasted_iota(jnp.int32, (2 * TR, PIX), 1)
    edge_want = jnp.where(edge_out < TR, edge_out * TC, (edge_out - TR) * TC + TC - 1)
    edge[...] = jnp.where(edge_src == edge_want, 1.0, 0.0).astype(BF)

    def columns(field):
        return jnp.dot(edge[...], field, preferred_element_type=F32).astype(BF)

    def rims(slots, tile_buf, col_buf, dst, dst_t, section, send_sem, recv_sem):
        for (delta_row, delta_col), slot in slots.items():
            if delta_row == -1:
                piece = tile_buf.at[TR - 1]
            elif delta_row == 1:
                piece = tile_buf.at[0]
            elif delta_col == -1:
                piece = col_buf.at[1]
            else:
                piece = col_buf.at[0]
            pltpu.make_async_remote_copy(
                src_ref=piece,
                dst_ref=dst.at[dst_t, slot],
                send_sem=send_sem,
                recv_sem=recv_sem,
                device_id={"section": section, "tile": at(-delta_row, -delta_col)},
                device_id_type=MESH,
            ).start()

    def wait_for(buf, sem):
        pltpu.make_async_copy(buf, buf, sem).wait()

    def turn_cotangent():
        def turn(t, carry):
            cot_t[t] = cot_ref[t].astype(F32).T
            return carry

        lax.fori_loop(0, STEPS, turn, 0)

    hin[0] = jnp.zeros((SLOTS, TC, CH), BF)
    for win in (win_f, win_b):
        rim = jnp.zeros((TC, win.shape[1]), BF)
        win[0:TC, :] = rim
        win[TC + PIX : EXT, :] = rim

    @pl.when(first)
    def _():
        def place(t, carry):
            field = frames_ref[t].astype(F32).T.astype(BF)
            xin[t, 0:TR] = field.reshape(TR, TC, CH)
            fcol[t] = columns(field).reshape(2, TR, CH)
            return carry

        lax.fori_loop(0, STEPS, place, 0)

    @pl.when(sec > 0)
    def _():
        turn_cotangent()

    pl.semaphore_wait(
        barrier,
        8 + jnp.where(last, 0, 9) + jnp.where(first, 0, 1),
    )

    @pl.when(first)
    def _():
        def share(t, carry):
            rims(FAR_SLOTS, xin.at[t], fcol.at[t], xin, t, sec, xs_sem.at[t], x_sem.at[STEPS + t])
            rims(NEAR_SLOTS, xin.at[t], fcol.at[t], xin, t, sec, xs_sem.at[t], x_sem.at[t])
            return carry

        lax.fori_loop(0, STEPS, share, 0)

    for copy in copies[0::2]:
        copy.wait()

    def spread(buf, t, width, win, base, stride):
        whole = buf[t, 0:NEAR].reshape(NEAR * TC, width)
        for side in range(2):
            moved = jnp.dot(pick[side], whole, preferred_element_type=F32).astype(BF)
            win[TC : TC + PIX, pl.ds(2 * side * stride + base, width)] = moved
        win[TC : TC + PIX, pl.ds(stride + base, width)] = whole[:PIX]

    def spread_far(buf, t, width, win, base, stride):
        whole = buf[t, NEAR:SLOTS].reshape(FAR * TC, width)
        for b in range(3):
            moved = jnp.dot(pick_far[b], whole, preferred_element_type=F32).astype(BF)
            win[:, pl.ds(b * stride + base, width)] = moved

    cells[0] = jnp.zeros((PIX, CH), F32)

    def send_rows(buf, buf_t, dst, dst_t, start, count, section, send_sem, recv_sem):
        pltpu.make_async_remote_copy(
            src_ref=buf.at[buf_t, pl.ds(start, count)],
            dst_ref=dst.at[dst_t, pl.ds(start, count)],
            send_sem=send_sem,
            recv_sem=recv_sem,
            device_id={"section": section, "tile": tile},
            device_id_type=MESH,
        ).start()

    def advance(t, low, high):
        z = z_ref[low:high, :]
        in_gate = jax.nn.sigmoid(z[:, :CH])
        forget = jax.nn.sigmoid(z[:, CH : 2 * CH])
        cand = jnp.tanh(z[:, 2 * CH : 3 * CH])
        out_gate = jax.nn.sigmoid(z[:, 3 * CH :])
        cell = forget * cells[t, low:high, :] + in_gate * cand
        hidden = (out_gate * jnp.tanh(cell)).astype(BF)
        hin[t + 1, low // TC : high // TC] = hidden.reshape((high - low) // TC, TC, CH)
        gates[t, low:high, 0:CH] = in_gate
        gates[t, low:high, CH : 2 * CH] = forget
        gates[t, low:high, 2 * CH : 3 * CH] = cand
        gates[t, low:high, 3 * CH :] = out_gate
        cells[t + 1, low:high, :] = cell

    def forward(t, carry):
        @pl.when(t > 0)
        def _():
            wait_for(hin.at[t, pl.ds(TR, 2)], h_sem.at[t])

        spread(hin, t, CH, win_f, CH, 2 * CH)

        @pl.when(first)
        def _():
            wait_for(xin.at[t, pl.ds(TR, 2)], x_sem.at[t])

        @pl.when(sec > 0)
        def _():
            wait_for(xin.at[t, pl.ds(0, NEAR)], x_sem.at[t])

        spread(xin, t, CH, win_f, 0, 2 * CH)
        z = bias_ref[...]
        for a in range(3):
            z = z + lax.dot_general(
                win_f[a * TC : a * TC + PIX, :],
                wf[a],
                (((1,), (1,)), ((), ())),
                preferred_element_type=F32,
            )
        z_ref[...] = z
        advance(t, TC, PIX - TC)

        @pl.when(sec < sections - 1)
        def _():
            send_rows(hin, t + 1, xin, t, 1, TR - 2, sec + 1, xs_sem.at[STEPS + t], x_sem.at[t])

        @pl.when(t > 0)
        def _():
            wait_for(hin.at[t, pl.ds(NEAR, FAR)], h_sem.at[STEPS + t])

        wait_for(xin.at[t, pl.ds(NEAR, FAR)], x_sem.at[STEPS + t])
        spread_far(hin, t, CH, far_f, CH, 2 * CH)
        spread_far(xin, t, CH, far_f, 0, 2 * CH)
        for a, start in ((0, 0), (2, PIX - TC)):
            far = far_f[0:TC, :] if a == 0 else far_f[TC : 2 * TC, :]
            z_ref[start : start + TC, :] += lax.dot_general(
                far, wf[a], (((1,), (1,)), ((), ())), preferred_element_type=F32
            )
        advance(t, 0, TC)
        advance(t, PIX - TC, PIX)

        @pl.when(sec < sections - 1)
        def _():
            rims(FAR_SLOTS, hin.at[t + 1], hcol.at[t], xin, t, sec + 1, xs_sem.at[STEPS + t], x_sem.at[STEPS + t])
            for edge_row in (0, TR - 1):
                send_rows(hin, t + 1, xin, t, edge_row, 1, sec + 1, xs_sem.at[STEPS + t], x_sem.at[t])

        @pl.when(t < STEPS - 1)
        def _():
            rims(FAR_SLOTS, hin.at[t + 1], hcol.at[t], hin, t + 1, sec, hs_sem.at[t], h_sem.at[STEPS + t + 1])

        field = hin[t + 1, 0:TR].reshape(PIX, CH)
        hcol[t] = columns(field).reshape(2, TR, CH)

        @pl.when(sec < sections - 1)
        def _():
            rims(NEAR_SLOTS, hin.at[t + 1], hcol.at[t], xin, t, sec + 1, xs_sem.at[STEPS + t], x_sem.at[t])

        @pl.when(t < STEPS - 1)
        def _():
            rims(NEAR_SLOTS, hin.at[t + 1], hcol.at[t], hin, t + 1, sec, hs_sem.at[t], h_sem.at[t + 1])

        hidden_ref[t] = field.astype(F32).T.astype(BF)
        return carry

    lax.fori_loop(0, STEPS, forward, 0)

    @pl.when(first)
    def _():
        turn_cotangent()

    for copy in copies[1::2]:
        copy.wait()

    def backward(back, carry):
        t = STEPS - 1 - back

        @pl.when(sec < sections - 1)
        def _():
            wait_for(din.at[t], d_sem.at[t])

        in_gate = gates[t, :, 0:CH]
        forget = gates[t, :, CH : 2 * CH]
        cand = gates[t, :, 2 * CH : 3 * CH]
        out_gate = gates[t, :, 3 * CH :]
        tanh_cell = jnp.tanh(cells[t + 1])
        d_hidden = cot_t[t] + din[t].reshape(PIX, CH).astype(F32) + du_ref[:, CH:]
        d_total = dc_ref[...] + d_hidden * out_gate * (1.0 - tanh_cell * tanh_cell)
        parts = [
            d_total * cand * in_gate * (1.0 - in_gate),
            d_total * cells[t] * forget * (1.0 - forget),
            d_total * in_gate * (1.0 - cand * cand),
            d_hidden * tanh_cell * out_gate * (1.0 - out_gate),
        ]
        dz = jnp.concatenate([part.astype(BF) for part in parts], 1)
        dc_ref[...] = d_total * forget
        dzin[t, 0:TR] = dz.reshape(TR, TC, 4 * CH)
        rims(FAR_SLOTS, dzin.at[t], dzcol.at[t], dzin, t, sec, dzs_sem.at[t], dz_sem.at[STEPS + t])
        dzcol[t] = columns(dz).reshape(2, TR, 4 * CH)
        rims(NEAR_SLOTS, dzin.at[t], dzcol.at[t], dzin, t, sec, dzs_sem.at[t], dz_sem.at[t])
        wait_for(dzin.at[t, pl.ds(TR, 2)], dz_sem.at[t])
        spread(dzin, t, 4 * CH, win_b, 0, 4 * CH)
        du = None
        for a in range(3):
            term = jnp.dot(
                win_b[(2 - a) * TC : (2 - a) * TC + PIX, :], wb[a], preferred_element_type=F32
            )
            du = term if du is None else du + term
        du_ref[...] = du
        dsend[t] = du[:, :CH].astype(BF).reshape(TR, TC, CH)
        above = (dsend, t, din, t)

        @pl.when(sec > 0)
        def _():
            send_rows(*above, 1, TR - 2, sec - 1, ds_sem.at[t], d_sem.at[t])

        wait_for(dzin.at[t, pl.ds(NEAR, FAR)], dz_sem.at[STEPS + t])
        spread_far(dzin, t, 4 * CH, far_b, 0, 4 * CH)
        for a, start in ((2, 0), (0, PIX - TC)):
            far = far_b[0:TC, :] if a == 2 else far_b[TC : 2 * TC, :]
            rim = du_ref[start : start + TC, :] + jnp.dot(far, wb[a], preferred_element_type=F32)
            du_ref[start : start + TC, :] = rim
            dsend[t, start // TC] = rim[:, :CH].astype(BF)

        @pl.when(sec > 0)
        def _():
            for edge_row in (0, TR - 1):
                send_rows(*above, edge_row, 1, sec - 1, ds_sem.at[t], d_sem.at[t])

        grads_ref[t] = du_ref[:, :CH].T.astype(BF)
        return carry

    @pl.when(last)
    def _():
        din[...] = jnp.zeros(din.shape, BF)

    du_ref[...] = jnp.zeros(du_ref.shape, F32)
    dc_ref[...] = jnp.zeros(dc_ref.shape, F32)
    lax.fori_loop(0, STEPS, backward, 0)

    def settle(t, carry):
        @pl.when(first)
        def _():
            wait_for(xin.at[t, pl.ds(0, 8)], xs_sem.at[t])

        @pl.when(sec < sections - 1)
        def _():
            wait_for(xin.at[t], xs_sem.at[STEPS + t])

        @pl.when(t < STEPS - 1)
        def _():
            wait_for(hin.at[t, pl.ds(0, 8)], hs_sem.at[t])

        wait_for(dzin.at[t, pl.ds(0, 8)], dzs_sem.at[t])

        @pl.when(sec > 0)
        def _():
            wait_for(dsend.at[t], ds_sem.at[t])

        return carry

    lax.fori_loop(0, STEPS, settle, 0)


def make_step(sections, tiles):
    def body(*refs):
        kernel(sections, tiles, *refs)

    return pl.pallas_call(
        body,
        out_shape=[jax.ShapeDtypeStruct((STEPS, CH, PIX), BF)] * 2,
        in_specs=[
            pl.BlockSpec(memory_space=pltpu.VMEM),
            pl.BlockSpec(memory_space=pl.ANY),
            pl.BlockSpec(memory_space=pltpu.VMEM),
            pl.BlockSpec(memory_space=pltpu.VMEM),
        ],
        out_specs=[pl.BlockSpec(memory_space=pltpu.VMEM)] * 2,
        scratch_shapes=[
            pltpu.VMEM((STEPS, SLOTS, TC, CH), BF),
            pltpu.VMEM((STEPS + 1, SLOTS, TC, CH), BF),
            pltpu.VMEM((STEPS, SLOTS, TC, 4 * CH), BF),
            pltpu.VMEM((STEPS, TR, TC, CH), BF),
            pltpu.VMEM((STEPS, 2, TR, CH), BF),
            pltpu.VMEM((STEPS, 2, TR, 4 * CH), BF),
            pltpu.VMEM((STEPS, TR, TC, CH), BF),
            pltpu.VMEM((STEPS, 2, TR, CH), BF),
            pltpu.VMEM((3, 4 * CH, 6 * CH), BF),
            pltpu.VMEM((3, 12 * CH, 2 * CH), BF),
            pltpu.VMEM((2, PIX, NEAR * TC), BF),
            pltpu.VMEM((3, 2 * TC, FAR * TC), BF),
            pltpu.VMEM((2 * TR, PIX), BF),
            pltpu.VMEM((EXT, 6 * CH), BF),
            pltpu.VMEM((EXT, 12 * CH), BF),
            pltpu.VMEM((2 * TC, 6 * CH), BF),
            pltpu.VMEM((2 * TC, 12 * CH), BF),
            pltpu.VMEM((PIX, 4 * CH), F32),
            pltpu.VMEM((PIX, 2 * CH), F32),
            pltpu.VMEM((PIX, CH), F32),
            pltpu.VMEM((STEPS, PIX, 4 * CH), F32),
            pltpu.VMEM((STEPS + 1, PIX, CH), F32),
            pltpu.VMEM((STEPS, PIX, CH), F32),
            pltpu.SemaphoreType.DMA((2 * STEPS,)),
            pltpu.SemaphoreType.DMA((2 * STEPS,)),
            pltpu.SemaphoreType.DMA((2 * STEPS,)),
            pltpu.SemaphoreType.DMA((STEPS,)),
            pltpu.SemaphoreType.DMA((2 * STEPS,)),
            pltpu.SemaphoreType.DMA((STEPS,)),
            pltpu.SemaphoreType.DMA((STEPS,)),
            pltpu.SemaphoreType.DMA((STEPS,)),
            pltpu.SemaphoreType.DMA((2, 9)),
        ],
        compiler_params=pltpu.CompilerParams(
            collective_id=0, has_side_effects=True, vmem_limit_bytes=56 * 1024 * 1024
        ),
        name="conv_lstm",
    )


def solution(mesh):
    step = make_step(mesh.shape["section"], mesh.shape["tile"])

    def per_device(frames, weights, gate_bias, cotangent):
        hidden, grads = step(
            frames.reshape(STEPS, CH, PIX), weights[0], gate_bias, cotangent.reshape(STEPS, CH, PIX)
        )
        shape = (1, STEPS, CH, 1, PIX)
        return hidden.reshape(shape), grads.reshape(shape)

    in_specs = (
        P(None, None, "tile", None),
        P("section", None, None, None),
        P("section", None),
        P("section", None, None, "tile", None),
    )
    out_specs = (P("section", None, None, "tile", None), P("section", None, None, "tile", None))
    return jax.shard_map(
        per_device, mesh=mesh, in_specs=in_specs, out_specs=out_specs, check_vma=False
    )
```

time: 214 us -> 196 us (0.916)
  Pallas kernels: 210 us -> 191 us
    pallas_call x1, Pallas kernels: 210 us -> 191 us  [per_device(): step(frames.reshape(STEPS, CH, PIX), weights[0], gate_bias, cotangent.res...]
where the time goes in v2:
time: 196 us; the launch traced here: 195 us
  Pallas kernels  191 us (97%)
  local copies, waits for them, and re-layouts  3.34 us (2%)
    pallas_call x1, Pallas kernels, per_device(): step(frames.reshape(STEPS, CH, PIX), weights[0], gate_bias, cotangent.res...  191 us

profile of v2, /device:TPU:6, one launch (start us, length us, event | category | flops | bytes accessed | tf_op | source)
XLA Modules:
  0.0 194.6 jit_solution(1667218548721998584)
XLA Ops:
  0.6 190.6 %conv_lstm.1 = (bf16[4,128,256]{2,1,0:T(8,128)(2,1)}, bf16[4,128,256]{2,1,0:T(8,128)(2,1)}) custom-call(bf16[4,128,256]{2,1,0:T(8,128)(2,1)} %bitcast.10, bf16[9,512,256]{2,1,0:T(8,128)(2,1)} %bitcast.9, f32[1,512]{1,0:T(1,128)} %refs_2_.1, bf16[4,128,256]{2,1,0:T(8,128)(2,1)} %bitcast.11), custom_call_target="tpu_custom_call" | custom-call | tf_op jit(solution)/shard_map/conv_lstm/pallas_call | solution.py:494
  191.2 1.7 copy.10
  192.9 1.7 copy.11

commit v3 on v2

v3 whole, which is shorter than its diff:
```python
import jax
import jax.numpy as jnp
from jax import lax
from jax.experimental import pallas as pl
from jax.experimental.pallas import tpu as pltpu
from jax.sharding import PartitionSpec as P

TG = 8
TR = 16
TC = 16
CH = 128
STEPS = 4
PIX = TR * TC
EXT = (TR + 2) * TC
SLOTS = TR + 4
MESH = pl.DeviceIdType.MESH
BF = jnp.bfloat16
F32 = jnp.float32

NEAR = TR + 2
FAR_DELTAS = ((-1, -1), (-1, 1), (1, -1), (1, 1), (-1, 0), (1, 0))
NEAR_DELTAS = ((0, -1), (0, 1))
DELTAS = FAR_DELTAS + NEAR_DELTAS


def kernel(
    sections,
    tiles,
    frames_ref,
    weights_ref,
    bias_ref,
    cot_ref,
    hidden_ref,
    grads_ref,
    xin,
    hin,
    dzin,
    din,
    hcol,
    dzcol,
    hcor,
    fcor,
    zcor,
    xcin,
    hcin,
    zcin,
    dsend,
    fcol,
    wf,
    wb,
    pick,
    pick_far,
    edge,
    win_f,
    win_b,
    far_f,
    far_b,
    z_ref,
    du_ref,
    dc_ref,
    gates,
    cells,
    cot_t,
    x_sem,
    h_sem,
    dz_sem,
    xt_sem,
    d_sem,
    fs_sem,
    xs_sem,
    hs_sem,
    xts_sem,
    dzs_sem,
    ds_sem,
    w_sem,
):
    sec = lax.axis_index("section")
    tile = lax.axis_index("tile")
    grid_rows = tiles // TG
    row = lax.div(tile, TG)
    col = lax.rem(tile, TG)
    first = sec == 0
    last = sec == sections - 1

    def at(delta_row, delta_col):
        there_row = lax.rem(row + (delta_row + grid_rows), grid_rows)
        there_col = lax.rem(col + (delta_col + TG), TG)
        return there_row * TG + there_col

    copies = []
    for a in range(3):
        for b in range(3):
            copies.append(
                pltpu.make_async_copy(
                    weights_ref.at[3 * a + b], wf.at[a, :, pl.ds(2 * CH * b, 2 * CH)], w_sem.at[0, 3 * a + b]
                )
            )
            copies.append(
                pltpu.make_async_copy(
                    weights_ref.at[3 * a + 2 - b], wb.at[a, pl.ds(4 * CH * b, 4 * CH), :], w_sem.at[1, 3 * a + b]
                )
            )
    for copy in copies:
        copy.start()

    hin[0] = jnp.zeros(hin.shape[1:], BF)
    for buf in (xin, hin, dzin):
        buf[:, TR:SLOTS] = jnp.zeros((buf.shape[0], SLOTS - TR, TC, buf.shape[3]), BF)
    for buf in (xcin, hcin, zcin):
        buf[...] = jnp.zeros(buf.shape, F32)

    barrier = pltpu.get_barrier_semaphore()
    for delta in DELTAS:
        pl.semaphore_signal(barrier, inc=1, device_id={"section": sec, "tile": at(*delta)}, device_id_type=MESH)

    @pl.when(sec > 0)
    def _():
        for delta in DELTAS:
            pl.semaphore_signal(
                barrier, inc=1, device_id={"section": sec - 1, "tile": at(*delta)}, device_id_type=MESH
            )
        pl.semaphore_signal(barrier, inc=1, device_id={"section": sec - 1, "tile": tile}, device_id_type=MESH)

    @pl.when(sec < sections - 1)
    def _():
        pl.semaphore_signal(barrier, inc=1, device_id={"section": sec + 1, "tile": tile}, device_id_type=MESH)

    def exists(delta_row, delta_col):
        seen = jnp.bool_(True)
        if delta_row:
            seen = row > 0 if delta_row < 0 else row < grid_rows - 1
        if delta_col:
            seen_col = col > 0 if delta_col < 0 else col < TG - 1
            seen = seen & seen_col if delta_row else seen_col
        return seen

    out_at = lax.broadcasted_iota(jnp.int32, (PIX, NEAR * TC), 0)
    src_at = lax.broadcasted_iota(jnp.int32, (PIX, NEAR * TC), 1)
    r_at = lax.shift_right_logical(out_at, 4)
    q_at = lax.bitwise_and(out_at, TC - 1)
    for side in range(2):
        on_rim = q_at == (0 if side == 0 else TC - 1)
        source = jnp.where(on_rim, (TR + side) * TC + r_at, out_at + (2 * side - 1))
        pick[side] = jnp.where(src_at == source, 1.0, 0.0).astype(BF)
    out_at = lax.broadcasted_iota(jnp.int32, (2 * TC, 2 * TC), 0)
    src_at = lax.broadcasted_iota(jnp.int32, (2 * TC, 2 * TC), 1)
    for side in range(2):
        pick_far[side] = jnp.where(src_at == out_at + (2 * side - 1), 1.0, 0.0).astype(BF)
    edge_out = lax.broadcasted_iota(jnp.int32, (2 * TR, PIX), 0)
    edge_src = lax.broadcasted_iota(jnp.int32, (2 * TR, PIX), 1)
    edge_want = jnp.where(edge_out < TR, edge_out * TC, (edge_out - TR) * TC + TC - 1)
    edge[...] = jnp.where(edge_src == edge_want, 1.0, 0.0).astype(BF)

    def columns(field):
        return jnp.dot(edge[...], field, preferred_element_type=F32).astype(BF)

    def rims(deltas, tile_buf, col_buf, cor_buf, dst, dst_cor, section, send_sem, recv_sem):
        for delta_row, delta_col in deltas:
            k = DELTAS.index((delta_row, delta_col))
            if k < 4:
                piece, there = cor_buf.at[3 - k], dst_cor.at[k]
            elif delta_row:
                piece = tile_buf.at[TR - 1 if delta_row < 0 else 0]
                there = dst.at[18 if delta_row < 0 else 19]
            else:
                piece = col_buf.at[1 if delta_col < 0 else 0]
                there = dst.at[16 if delta_col < 0 else 17]

            @pl.when(exists(-delta_row, -delta_col))
            def _():
                pltpu.make_async_remote_copy(
                    src_ref=piece,
                    dst_ref=there,
                    send_sem=send_sem.at[k],
                    recv_sem=recv_sem.at[k],
                    device_id={"section": section, "tile": at(-delta_row, -delta_col)},
                    device_id_type=MESH,
                ).start()

    def settle_rims(deltas, buf, cor, sems, sign=1):
        for delta_row, delta_col in deltas:
            k = DELTAS.index((delta_row, delta_col))

            @pl.when(exists(sign * delta_row, sign * delta_col))
            def _():
                wait_for(cor.at[k] if k < 4 else buf.at[TR], sems.at[k])

    def set_corners(cor, top, low):
        cor[0] = top[0:1].astype(F32)
        cor[1] = top[TC - 1 : TC].astype(F32)
        cor[2] = low[0:1].astype(F32)
        cor[3] = low[TC - 1 : TC].astype(F32)

    def wait_for(buf, sem):
        pltpu.make_async_copy(buf, buf, sem).wait()

    def turn_cotangent():
        def turn(t, carry):
            cot_t[t] = cot_ref[t].astype(F32).T
            return carry

        lax.fori_loop(0, STEPS, turn, 0)

    for win in (win_f, win_b):
        rim = jnp.zeros((TC, win.shape[1]), BF)
        win[0:TC, :] = rim
        win[TC + PIX : EXT, :] = rim

    @pl.when(first)
    def _():
        def place(t, carry):
            field = frames_ref[t].astype(F32).T.astype(BF)
            xin[t, 0:TR] = field.reshape(TR, TC, CH)
            fcol[t] = columns(field).reshape(2, TR, CH)
            set_corners(fcor.at[t], field[:TC].astype(F32), field[PIX - TC :].astype(F32))
            return carry

        lax.fori_loop(0, STEPS, place, 0)

    @pl.when(sec > 0)
    def _():
        turn_cotangent()

    pl.semaphore_wait(
        barrier,
        8 + jnp.where(last, 0, 9) + jnp.where(first, 0, 1),
    )

    @pl.when(first)
    def _():
        def share(t, carry):
            rims(DELTAS, xin.at[t], fcol.at[t], fcor.at[t], xin.at[t], xcin.at[t], sec, fs_sem.at[t], x_sem.at[t])
            return carry

        lax.fori_loop(0, STEPS, share, 0)

    for copy in copies[0::2]:
        copy.wait()

    def spread(buf, t, width, win, base, stride):
        whole = buf[t, 0:NEAR].reshape(NEAR * TC, width)
        for side in range(2):
            moved = jnp.dot(pick[side], whole, preferred_element_type=F32).astype(BF)
            win[TC : TC + PIX, pl.ds(2 * side * stride + base, width)] = moved
        win[TC : TC + PIX, pl.ds(stride + base, width)] = whole[:PIX]

    def spread_far(buf, cor, t, width, win, base, stride):
        whole = buf[t, NEAR:SLOTS].reshape(2 * TC, width)
        q_at = lax.broadcasted_iota(jnp.int32, (TC, width), 0)
        for side in range(2):
            moved = jnp.dot(pick_far[side], whole, preferred_element_type=F32)
            rim = q_at == (0 if side == 0 else TC - 1)
            for low in range(2):
                cell = jnp.broadcast_to(cor[t, 2 * low + side], (TC, width))
                part = jnp.where(rim, cell, moved[low * TC : (low + 1) * TC])
                win[low * TC : (low + 1) * TC, pl.ds(2 * side * stride + base, width)] = part.astype(BF)
        win[:, pl.ds(stride + base, width)] = whole

    cells[0] = jnp.zeros((PIX, CH), F32)

    def send_rows(buf, buf_t, dst, dst_t, start, count, section, send_sem, recv_sem):
        pltpu.make_async_remote_copy(
            src_ref=buf.at[buf_t, pl.ds(start, count)],
            dst_ref=dst.at[dst_t, pl.ds(start, count)],
            send_sem=send_sem,
            recv_sem=recv_sem,
            device_id={"section": section, "tile": tile},
            device_id_type=MESH,
        ).start()

    def advance(t, low, high):
        z = z_ref[low:high, :]
        in_gate = jax.nn.sigmoid(z[:, :CH])
        forget = jax.nn.sigmoid(z[:, CH : 2 * CH])
        cand = jnp.tanh(z[:, 2 * CH : 3 * CH])
        out_gate = jax.nn.sigmoid(z[:, 3 * CH :])
        cell = forget * cells[t, low:high, :] + in_gate * cand
        hidden = (out_gate * jnp.tanh(cell)).astype(BF)
        hin[t + 1, low // TC : high // TC] = hidden.reshape((high - low) // TC, TC, CH)
        gates[t, low:high, 0:CH] = in_gate
        gates[t, low:high, CH : 2 * CH] = forget
        gates[t, low:high, 2 * CH : 3 * CH] = cand
        gates[t, low:high, 3 * CH :] = out_gate
        cells[t + 1, low:high, :] = cell
        return hidden.astype(F32)

    def forward(t, carry):
        @pl.when(t > 0)
        def _():
            settle_rims(NEAR_DELTAS, hin.at[t], hcin.at[t], h_sem.at[t])

        spread(hin, t, CH, win_f, CH, 2 * CH)

        @pl.when(sec > 0)
        def _():
            wait_for(xin.at[t, pl.ds(1, TR - 2)], xt_sem.at[t, 0])
            wait_for(xin.at[t, pl.ds(0, 2)], xt_sem.at[t, 1])

        settle_rims(NEAR_DELTAS, xin.at[t], xcin.at[t], x_sem.at[t])
        spread(xin, t, CH, win_f, 0, 2 * CH)
        z = bias_ref[...]
        for a in range(3):
            z = z + lax.dot_general(
                win_f[a * TC : a * TC + PIX, :],
                wf[a],
                (((1,), (1,)), ((), ())),
                preferred_element_type=F32,
            )
        z_ref[...] = z
        advance(t, TC, PIX - TC)

        @pl.when(sec < sections - 1)
        def _():
            send_rows(hin, t + 1, xin, t, 1, TR - 2, sec + 1, xts_sem.at[t, 0], xt_sem.at[t, 0])

        @pl.when(t > 0)
        def _():
            settle_rims(FAR_DELTAS, hin.at[t], hcin.at[t], h_sem.at[t])

        settle_rims(FAR_DELTAS, xin.at[t], xcin.at[t], x_sem.at[t])
        spread_far(hin, hcin, t, CH, far_f, CH, 2 * CH)
        spread_far(xin, xcin, t, CH, far_f, 0, 2 * CH)
        for a, start in ((0, 0), (2, PIX - TC)):
            far = far_f[0:TC, :] if a == 0 else far_f[TC : 2 * TC, :]
            z_ref[start : start + TC, :] += lax.dot_general(
                far, wf[a], (((1,), (1,)), ((), ())), preferred_element_type=F32
            )
        top = advance(t, 0, TC)
        low = advance(t, PIX - TC, PIX)
        set_corners(hcor.at[t], top, low)

        def share(deltas):
            @pl.when(sec < sections - 1)
            def _():
                rims(
                    deltas, hin.at[t + 1], hcol.at[t], hcor.at[t], xin.at[t], xcin.at[t], sec + 1, xs_sem.at[t], x_sem.at[t]
                )

            @pl.when(t < STEPS - 1)
            def _():
                rims(
                    deltas,
                    hin.at[t + 1],
                    hcol.at[t],
                    hcor.at[t],
                    hin.at[t + 1],
                    hcin.at[t + 1],
                    sec,
                    hs_sem.at[t],
                    h_sem.at[t + 1],
                )

        share(FAR_DELTAS)

        @pl.when(sec < sections - 1)
        def _():
            for edge_row in (0, TR - 1):
                send_rows(hin, t + 1, xin, t, edge_row, 1, sec + 1, xts_sem.at[t, 1], xt_sem.at[t, 1])

        field = hin[t + 1, 0:TR].reshape(PIX, CH)
        hcol[t] = columns(field).reshape(2, TR, CH)
        share(NEAR_DELTAS)
        hidden_ref[t] = field.astype(F32).T.astype(BF)
        return carry

    lax.fori_loop(0, STEPS, forward, 0)

    @pl.when(first)
    def _():
        turn_cotangent()

    for copy in copies[1::2]:
        copy.wait()

    def slope(t, low, high):
        in_gate = gates[t, low:high, 0:CH]
        forget = gates[t, low:high, CH : 2 * CH]
        cand = gates[t, low:high, 2 * CH : 3 * CH]
        out_gate = gates[t, low:high, 3 * CH :]
        tanh_cell = jnp.tanh(cells[t + 1, low:high, :])
        rows = (high - low) // TC
        from_above = din[t, low // TC : high // TC].reshape(high - low, CH).astype(F32)
        d_hidden = cot_t[t, low:high, :] + from_above + du_ref[low:high, CH:]
        d_total = dc_ref[low:high, :] + d_hidden * out_gate * (1.0 - tanh_cell * tanh_cell)
        parts = [
            d_total * cand * in_gate * (1.0 - in_gate),
            d_total * cells[t, low:high, :] * forget * (1.0 - forget),
            d_total * in_gate * (1.0 - cand * cand),
            d_hidden * tanh_cell * out_gate * (1.0 - out_gate),
        ]
        dz = jnp.concatenate([part.astype(BF) for part in parts], 1)
        dc_ref[low:high, :] = d_total * forget
        dzin[t, low // TC : high // TC] = dz.reshape(rows, TC, 4 * CH)
        return dz.astype(F32)

    def backward(back, carry):
        t = STEPS - 1 - back

        @pl.when(sec < sections - 1)
        def _():
            wait_for(din.at[t, pl.ds(1, TR - 2)], d_sem.at[t, 0])

        slope(t, TC, PIX - TC)

        @pl.when(sec < sections - 1)
        def _():
            wait_for(din.at[t, pl.ds(0, 2)], d_sem.at[t, 1])

        top = slope(t, 0, TC)
        low = slope(t, PIX - TC, PIX)
        set_corners(zcor.at[t], top, low)

        def share(deltas):
            rims(
                deltas, dzin.at[t], dzcol.at[t], zcor.at[t], dzin.at[t], zcin.at[t], sec, dzs_sem.at[t], dz_sem.at[t]
            )

        share(FAR_DELTAS)
        dzcol[t] = columns(dzin[t, 0:TR].reshape(PIX, 4 * CH)).reshape(2, TR, 4 * CH)
        share(NEAR_DELTAS)
        settle_rims(NEAR_DELTAS, dzin.at[t], zcin.at[t], dz_sem.at[t])
        spread(dzin, t, 4 * CH, win_b, 0, 4 * CH)
        du = None
        for a in range(3):
            term = jnp.dot(
                win_b[(2 - a) * TC : (2 - a) * TC + PIX, :], wb[a], preferred_element_type=F32
            )
            du = term if du is None else du + term
        du_ref[...] = du
        dsend[t] = du[:, :CH].astype(BF).reshape(TR, TC, CH)
        above = (dsend, t, din, t)

        @pl.when(sec > 0)
        def _():
            send_rows(*above, 1, TR - 2, sec - 1, ds_sem.at[t, 0], d_sem.at[t, 0])

        settle_rims(FAR_DELTAS, dzin.at[t], zcin.at[t], dz_sem.at[t])
        spread_far(dzin, zcin, t, 4 * CH, far_b, 0, 4 * CH)
        for a, start in ((2, 0), (0, PIX - TC)):
            far = far_b[0:TC, :] if a == 2 else far_b[TC : 2 * TC, :]
            rim = du_ref[start : start + TC, :] + jnp.dot(far, wb[a], preferred_element_type=F32)
            du_ref[start : start + TC, :] = rim
            dsend[t, start // TC] = rim[:, :CH].astype(BF)

        @pl.when(sec > 0)
        def _():
            for edge_row in (0, TR - 1):
                send_rows(*above, edge_row, 1, sec - 1, ds_sem.at[t, 1], d_sem.at[t, 1])

        grads_ref[t] = du_ref[:, :CH].T.astype(BF)
        return carry

    @pl.when(last)
    def _():
        din[...] = jnp.zeros(din.shape, BF)

    du_ref[...] = jnp.zeros(du_ref.shape, F32)
    dc_ref[...] = jnp.zeros(dc_ref.shape, F32)
    lax.fori_loop(0, STEPS, backward, 0)

    def settle(t, carry):
        @pl.when(first)
        def _():
            settle_rims(DELTAS, xin.at[t], xcin.at[t], fs_sem.at[t], -1)

        @pl.when(sec < sections - 1)
        def _():
            settle_rims(DELTAS, xin.at[t], xcin.at[t], xs_sem.at[t], -1)
            wait_for(xin.at[t, pl.ds(1, TR - 2)], xts_sem.at[t, 0])
            wait_for(xin.at[t, pl.ds(0, 2)], xts_sem.at[t, 1])

        @pl.when(t < STEPS - 1)
        def _():
            settle_rims(DELTAS, hin.at[t], hcin.at[t], hs_sem.at[t], -1)

        settle_rims(DELTAS, dzin.at[t], zcin.at[t], dzs_sem.at[t], -1)

        @pl.when(sec > 0)
        def _():
            wait_for(dsend.at[t, pl.ds(1, TR - 2)], ds_sem.at[t, 0])
            wait_for(dsend.at[t, pl.ds(0, 2)], ds_sem.at[t, 1])

        return carry

    lax.fori_loop(0, STEPS, settle, 0)


def make_step(sections, tiles):
    def body(*refs):
        kernel(sections, tiles, *refs)

    return pl.pallas_call(
        body,
        out_shape=[jax.ShapeDtypeStruct((STEPS, CH, PIX), BF)] * 2,
        in_specs=[
            pl.BlockSpec(memory_space=pltpu.VMEM),
            pl.BlockSpec(memory_space=pl.ANY),
            pl.BlockSpec(memory_space=pltpu.VMEM),
            pl.BlockSpec(memory_space=pltpu.VMEM),
        ],
        out_specs=[pl.BlockSpec(memory_space=pltpu.VMEM)] * 2,
        scratch_shapes=[
            pltpu.VMEM((STEPS, SLOTS, TC, CH), BF),
            pltpu.VMEM((STEPS + 1, SLOTS, TC, CH), BF),
            pltpu.VMEM((STEPS, SLOTS, TC, 4 * CH), BF),
            pltpu.VMEM((STEPS, TR, TC, CH), BF),
            pltpu.VMEM((STEPS, 2, TR, CH), BF),
            pltpu.VMEM((STEPS, 2, TR, 4 * CH), BF),
            pltpu.VMEM((STEPS, 4, 1, CH), F32),
            pltpu.VMEM((STEPS, 4, 1, CH), F32),
            pltpu.VMEM((STEPS, 4, 1, 4 * CH), F32),
            pltpu.VMEM((STEPS, 4, 1, CH), F32),
            pltpu.VMEM((STEPS, 4, 1, CH), F32),
            pltpu.VMEM((STEPS, 4, 1, 4 * CH), F32),
            pltpu.VMEM((STEPS, TR, TC, CH), BF),
            pltpu.VMEM((STEPS, 2, TR, CH), BF),
            pltpu.VMEM((3, 4 * CH, 6 * CH), BF),
            pltpu.VMEM((3, 12 * CH, 2 * CH), BF),
            pltpu.VMEM((2, PIX, NEAR * TC), BF),
            pltpu.VMEM((2, 2 * TC, 2 * TC), BF),
            pltpu.VMEM((2 * TR, PIX), BF),
            pltpu.VMEM((EXT, 6 * CH), BF),
            pltpu.VMEM((EXT, 12 * CH), BF),
            pltpu.VMEM((2 * TC, 6 * CH), BF),
            pltpu.VMEM((2 * TC, 12 * CH), BF),
            pltpu.VMEM((PIX, 4 * CH), F32),
            pltpu.VMEM((PIX, 2 * CH), F32),
            pltpu.VMEM((PIX, CH), F32),
            pltpu.VMEM((STEPS, PIX, 4 * CH), F32),
            pltpu.VMEM((STEPS + 1, PIX, CH), F32),
            pltpu.VMEM((STEPS, PIX, CH), F32),
            pltpu.SemaphoreType.DMA((STEPS, 8)),
            pltpu.SemaphoreType.DMA((STEPS, 8)),
            pltpu.SemaphoreType.DMA((STEPS, 8)),
            pltpu.SemaphoreType.DMA((STEPS, 2)),
            pltpu.SemaphoreType.DMA((STEPS, 2)),
            pltpu.SemaphoreType.DMA((STEPS, 8)),
            pltpu.SemaphoreType.DMA((STEPS, 8)),
            pltpu.SemaphoreType.DMA((STEPS, 8)),
            pltpu.SemaphoreType.DMA((STEPS, 2)),
            pltpu.SemaphoreType.DMA((STEPS, 8)),
            pltpu.SemaphoreType.DMA((STEPS, 2)),
            pltpu.SemaphoreType.DMA((2, 9)),
        ],
        compiler_params=pltpu.CompilerParams(
            collective_id=0, has_side_effects=True, vmem_limit_bytes=56 * 1024 * 1024
        ),
        name="conv_lstm",
    )


def solution(mesh):
    step = make_step(mesh.shape["section"], mesh.shape["tile"])

    def per_device(frames, weights, gate_bias, cotangent):
        hidden, grads = step(
            frames.reshape(STEPS, CH, PIX), weights[0], gate_bias, cotangent.reshape(STEPS, CH, PIX)
        )
        shape = (1, STEPS, CH, 1, PIX)
        return hidden.reshape(shape), grads.reshape(shape)

    in_specs = (
        P(None, None, "tile", None),
        P("section", None, None, None),
        P("section", None),
        P("section", None, None, "tile", None),
    )
    out_specs = (P("section", None, None, "tile", None), P("section", None, None, "tile", None))
    return jax.shard_map(
        per_device, mesh=mesh, in_specs=in_specs, out_specs=out_specs, check_vma=False
    )
```

time: 196 us -> 185 us (0.944)
  Pallas kernels: 191 us -> 181 us
    pallas_call x1, Pallas kernels: 191 us -> 181 us  [per_device(): step(frames.reshape(STEPS, CH, PIX), weights[0], gate_bias, cotangent.res...]
where the time goes in v3:
time: 185 us
  Pallas kernels  181 us (98%)
  local copies, waits for them, and re-layouts  3.34 us (2%)
    pallas_call x1, Pallas kernels, per_device(): step(frames.reshape(STEPS, CH, PIX), weights[0], gate_bias, cotangent.res...  181 us

profile of v3, /device:TPU:6, one launch (start us, length us, event | category | flops | bytes accessed | tf_op | source)
XLA Modules:
  0.0 184.8 jit_solution(15883914670472178825)
XLA Ops:
  0.6 180.8 %conv_lstm.1 = (bf16[4,128,256]{2,1,0:T(8,128)(2,1)}, bf16[4,128,256]{2,1,0:T(8,128)(2,1)}) custom-call(bf16[4,128,256]{2,1,0:T(8,128)(2,1)} %bitcast.10, bf16[9,512,256]{2,1,0:T(8,128)(2,1)} %bitcast.9, f32[1,512]{1,0:T(1,128)} %refs_2_.1, bf16[4,128,256]{2,1,0:T(8,128)(2,1)} %bitcast.11), custom_call_target="tpu_custom_call" | custom-call | tf_op jit(solution)/shard_map/conv_lstm/pallas_call | solution.py:556
  181.4 1.7 copy.10
  183.1 1.7 copy.11

commit v4 on v3

--- a/solution.py
+++ b/solution.py
@@ -44,6 +44,10 @@
     xcin,
     hcin,
     zcin,
+    frames_in,
+    cot_in,
+    stage,
+    land,
     dsend,
     fcol,
     wf,
@@ -73,11 +77,22 @@
     dzs_sem,
     ds_sem,
     w_sem,
+    fin_sem,
+    cin_sem,
+    out_sem,
 ):
     sec = lax.axis_index("section")
     tile = lax.axis_index("tile")
     grid_rows = tiles // TG
-    row = lax.div(tile, TG)
+    half = grid_rows // 2
+
+    def mirror(grid_row):
+        return jnp.where(grid_row >= half, half + grid_rows - 1 - grid_row, grid_row)
+
+    stored_row = lax.div(tile, TG)
+    swapped = stored_row >= half
+    kept = stored_row < half
+    row = mirror(stored_row)
     col = lax.rem(tile, TG)
     first = sec == 0
     last = sec == sections - 1
@@ -85,7 +100,9 @@
     def at(delta_row, delta_col):
         there_row = lax.rem(row + (delta_row + grid_rows), grid_rows)
         there_col = lax.rem(col + (delta_col + TG), TG)
-        return there_row * TG + there_col
+        return mirror(there_row) * TG + there_col
+
+    partner = {"section": sec, "tile": row * TG + col}
 
     copies = []
     for a in range(3):
@@ -133,6 +150,10 @@
             seen_col = col > 0 if delta_col < 0 else col < TG - 1
             seen = seen & seen_col if delta_row else seen_col
         return seen
+
+    @pl.when(swapped)
+    def _():
+        pl.semaphore_signal(barrier, inc=1, device_id=partner, device_id_type=MESH)
 
     out_at = lax.broadcasted_iota(jnp.int32, (PIX, NEAR * TC), 0)
     src_at = lax.broadcasted_iota(jnp.int32, (PIX, NEAR * TC), 1)
@@ -194,41 +215,82 @@
     def wait_for(buf, sem):
         pltpu.make_async_copy(buf, buf, sem).wait()
 
-    def turn_cotangent():
+    def turn_cotangent(source):
         def turn(t, carry):
-            cot_t[t] = cot_ref[t].astype(F32).T
+            cot_t[t] = source[t].astype(F32).T
             return carry
 
         lax.fori_loop(0, STEPS, turn, 0)
+
+    def to_partner(src, dst, send_sem, recv_sem):
+        return pltpu.make_async_remote_copy(
+            src_ref=src,
+            dst_ref=dst,
+            send_sem=send_sem,
+            recv_sem=recv_sem,
+            device_id=partner,
+            device_id_type=MESH,
+        )
+
+    def emit(which, out_ref, t, field):
+        value = field.reshape(PIX, CH).astype(F32).T.astype(BF)
+
+        @pl.when(swapped)
+        def _():
+            stage[which, t] = value
+            to_partner(stage.at[which, t], land.at[which, t], out_sem.at[0, which, t], out_sem.at[1, which, t]).start()
+
+        @pl.when(kept)
+        def _():
+            out_ref[t] = value
 
     for win in (win_f, win_b):
         rim = jnp.zeros((TC, win.shape[1]), BF)
         win[0:TC, :] = rim
         win[TC + PIX : EXT, :] = rim
 
-    @pl.when(first)
-    def _():
-        def place(t, carry):
-            field = frames_ref[t].astype(F32).T.astype(BF)
-            xin[t, 0:TR] = field.reshape(TR, TC, CH)
-            fcol[t] = columns(field).reshape(2, TR, CH)
-            set_corners(fcor.at[t], field[:TC].astype(F32), field[PIX - TC :].astype(F32))
+    def place(source, t):
+        field = source[t].astype(F32).T.astype(BF)
+        xin[t, 0:TR] = field.reshape(TR, TC, CH)
+        fcol[t] = columns(field).reshape(2, TR, CH)
+        set_corners(fcor.at[t], field[:TC].astype(F32), field[PIX - TC :].astype(F32))
+
+    @pl.when(first & kept)
+    def _():
+        def place_own(t, carry):
+            place(frames_ref, t)
             return carry
 
-        lax.fori_loop(0, STEPS, place, 0)
-
-    @pl.when(sec > 0)
-    def _():
-        turn_cotangent()
+        lax.fori_loop(0, STEPS, place_own, 0)
+
+    early = (sec > 0) & kept
+
+    @pl.when(early)
+    def _():
+        turn_cotangent(cot_ref)
 
     pl.semaphore_wait(
         barrier,
-        8 + jnp.where(last, 0, 9) + jnp.where(first, 0, 1),
+        8 + jnp.where(last, 0, 9) + jnp.where(first, 0, 1) + jnp.where(swapped, 1, 0),
     )
 
+    @pl.when(first & swapped)
+    def _():
+        for t in range(STEPS):
+            to_partner(frames_ref.at[t], frames_in.at[t], fin_sem.at[0, t], fin_sem.at[1, t]).start()
+
+    @pl.when(swapped)
+    def _():
+        to_partner(cot_ref, cot_in, cin_sem.at[0], cin_sem.at[1]).start()
+
     @pl.when(first)
     def _():
         def share(t, carry):
+            @pl.when(swapped)
+            def _():
+                wait_for(frames_in.at[t], fin_sem.at[1, t])
+                place(frames_in, t)
+
             rims(DELTAS, xin.at[t], fcol.at[t], fcor.at[t], xin.at[t], xcin.at[t], sec, fs_sem.at[t], x_sem.at[t])
             return carry
 
@@ -360,14 +422,18 @@
         field = hin[t + 1, 0:TR].reshape(PIX, CH)
         hcol[t] = columns(field).reshape(2, TR, CH)
         share(NEAR_DELTAS)
-        hidden_ref[t] = field.astype(F32).T.astype(BF)
         return carry
 
     lax.fori_loop(0, STEPS, forward, 0)
 
-    @pl.when(first)
-    def _():
-        turn_cotangent()
+    @pl.when(swapped)
+    def _():
+        wait_for(cot_in, cin_sem.at[1])
+        turn_cotangent(cot_in)
+
+    @pl.when(first & kept)
+    def _():
+        turn_cotangent(cot_ref)
 
     for copy in copies[1::2]:
         copy.wait()
@@ -418,6 +484,12 @@
         share(FAR_DELTAS)
         dzcol[t] = columns(dzin[t, 0:TR].reshape(PIX, 4 * CH)).reshape(2, TR, 4 * CH)
         share(NEAR_DELTAS)
+        emit(0, hidden_ref, t, hin[t + 1, 0:TR])
+
+        @pl.when(back > 0)
+        def _():
+            emit(1, grads_ref, t + 1, dsend[t + 1])
+
         settle_rims(NEAR_DELTAS, dzin.at[t], zcin.at[t], dz_sem.at[t])
         spread(dzin, t, 4 * CH, win_b, 0, 4 * CH)
         du = None
@@ -447,7 +519,6 @@
             for edge_row in (0, TR - 1):
                 send_rows(*above, edge_row, 1, sec - 1, ds_sem.at[t, 1], d_sem.at[t, 1])
 
-        grads_ref[t] = du_ref[:, :CH].T.astype(BF)
         return carry
 
     @pl.when(last)
@@ -457,6 +528,7 @@
     du_ref[...] = jnp.zeros(du_ref.shape, F32)
     dc_ref[...] = jnp.zeros(dc_ref.shape, F32)
     lax.fori_loop(0, STEPS, backward, 0)
+    emit(1, grads_ref, 0, dsend[0])
 
     def settle(t, carry):
         @pl.when(first)
@@ -483,6 +555,24 @@
         return carry
 
     lax.fori_loop(0, STEPS, settle, 0)
+
+    @pl.when(first & swapped)
+    def _():
+        for t in range(STEPS):
+            wait_for(frames_in.at[t], fin_sem.at[0, t])
+
+    @pl.when(swapped)
+    def _():
+        wait_for(cot_in, cin_sem.at[0])
+
+        def fetch(t, carry):
+            for which, out_ref in enumerate((hidden_ref, grads_ref)):
+                wait_for(stage.at[which, t], out_sem.at[0, which, t])
+                wait_for(land.at[which, t], out_sem.at[1, which, t])
+                out_ref[t] = land[which, t]
+            return carry
+
+        lax.fori_loop(0, STEPS, fetch, 0)
 
 
 def make_step(sections, tiles):
@@ -512,6 +602,10 @@
             pltpu.VMEM((STEPS, 4, 1, CH), F32),
             pltpu.VMEM((STEPS, 4, 1, CH), F32),
             pltpu.VMEM((STEPS, 4, 1, 4 * CH), F32),
+            pltpu.VMEM((STEPS, CH, PIX), BF),
+            pltpu.VMEM((STEPS, CH, PIX), BF),
+            pltpu.VMEM((2, STEPS, CH, PIX), BF),
+            pltpu.VMEM((2, STEPS, CH, PIX), BF),
             pltpu.VMEM((STEPS, TR, TC, CH), BF),
             pltpu.VMEM((STEPS, 2, TR, CH), BF),
             pltpu.VMEM((3, 4 * CH, 6 * CH), BF),
@@ -541,6 +635,9 @@
             pltpu.SemaphoreType.DMA((STEPS, 8)),
             pltpu.SemaphoreType.DMA((STEPS, 2)),
             pltpu.SemaphoreType.DMA((2, 9)),
+            pltpu.SemaphoreType.DMA((2, STEPS)),
+            pltpu.SemaphoreType.DMA((2,)),
+            pltpu.SemaphoreType.DMA((2, 2, STEPS)),
         ],
         compiler_params=pltpu.CompilerParams(
             collective_id=0, has_side_effects=True, vmem_limit_bytes=56 * 1024 * 1024

time: 185 us -> 167 us (0.903); the launches traced: 185 us -> 165 us
  Pallas kernels: 181 us -> 161 us
    pallas_call x1, Pallas kernels: 181 us -> 161 us  [per_device(): step(frames.reshape(STEPS, CH, PIX), weights[0], gate_bias, cotangent.res...]
where the time goes in v4:
time: 167 us; the launch traced here: 165 us
  Pallas kernels  161 us (96%)
  local copies, waits for them, and re-layouts  3.34 us (2%)
    pallas_call x1, Pallas kernels, per_device(): step(frames.reshape(STEPS, CH, PIX), weights[0], gate_bias, cotangent.res...  161 us

profile of v4, /device:TPU:6, one launch (start us, length us, event | category | flops | bytes accessed | tf_op | source)
XLA Modules:
  0.0 164.8 jit_solution(1590245169450017804)
XLA Ops:
  0.6 160.8 %conv_lstm.1 = (bf16[4,128,256]{2,1,0:T(8,128)(2,1)}, bf16[4,128,256]{2,1,0:T(8,128)(2,1)}) custom-call(bf16[4,128,256]{2,1,0:T(8,128)(2,1)} %bitcast.10, bf16[9,512,256]{2,1,0:T(8,128)(2,1)} %bitcast.9, f32[1,512]{1,0:T(1,128)} %refs_2_.1, bf16[4,128,256]{2,1,0:T(8,128)(2,1)} %bitcast.11), custom_call_target="tpu_custom_call" | custom-call | tf_op jit(solution)/shard_map/conv_lstm/pallas_call | solution.py:653
  161.4 1.7 %copy.10 = bf16[1,4,128,1,256]{4,2,3,1,0:T(8,128)(2,1)} copy(bf16[1,4,128,1,256]{4,2,3,1,0:T(8,128)(2,1)} %bitcast.13) | data formatting | bytes 524288
  163.1 1.7 %copy.11 = bf16[1,4,128,1,256]{4,2,3,1,0:T(8,128)(2,1)} copy(bf16[1,4,128,1,256]{4,2,3,1,0:T(8,128)(2,1)} %bitcast.12) | data formatting | bytes 524288

commit v5 on v4

--- a/solution.py
+++ b/solution.py
@@ -20,6 +20,8 @@
 NEAR = TR + 2
 FAR_DELTAS = ((-1, -1), (-1, 1), (1, -1), (1, 1), (-1, 0), (1, 0))
 NEAR_DELTAS = ((0, -1), (0, 1))
+ABOVE = ((-1, -1), (-1, 1), (-1, 0))
+BELOW = ((1, -1), (1, 1), (1, 0))
 DELTAS = FAR_DELTAS + NEAR_DELTAS
 
 
@@ -163,8 +165,8 @@
         on_rim = q_at == (0 if side == 0 else TC - 1)
         source = jnp.where(on_rim, (TR + side) * TC + r_at, out_at + (2 * side - 1))
         pick[side] = jnp.where(src_at == source, 1.0, 0.0).astype(BF)
-    out_at = lax.broadcasted_iota(jnp.int32, (2 * TC, 2 * TC), 0)
-    src_at = lax.broadcasted_iota(jnp.int32, (2 * TC, 2 * TC), 1)
+    out_at = lax.broadcasted_iota(jnp.int32, (TC, TC), 0)
+    src_at = lax.broadcasted_iota(jnp.int32, (TC, TC), 1)
     for side in range(2):
         pick_far[side] = jnp.where(src_at == out_at + (2 * side - 1), 1.0, 0.0).astype(BF)
     edge_out = lax.broadcasted_iota(jnp.int32, (2 * TR, PIX), 0)
@@ -206,11 +208,20 @@
             def _():
                 wait_for(cor.at[k] if k < 4 else buf.at[TR], sems.at[k])
 
-    def set_corners(cor, top, low):
-        cor[0] = top[0:1].astype(F32)
-        cor[1] = top[TC - 1 : TC].astype(F32)
-        cor[2] = low[0:1].astype(F32)
-        cor[3] = low[TC - 1 : TC].astype(F32)
+    def set_corners(cor, side, rim):
+        cor[2 * side] = rim[0:1]
+        cor[2 * side + 1] = rim[TC - 1 : TC]
+
+    def both_sides(work):
+        @pl.when(kept)
+        def _():
+            work(0)
+            work(1)
+
+        @pl.when(swapped)
+        def _():
+            work(1)
+            work(0)
 
     def wait_for(buf, sem):
         pltpu.make_async_copy(buf, buf, sem).wait()
@@ -253,7 +264,8 @@
         field = source[t].astype(F32).T.astype(BF)
         xin[t, 0:TR] = field.reshape(TR, TC, CH)
         fcol[t] = columns(field).reshape(2, TR, CH)
-        set_corners(fcor.at[t], field[:TC].astype(F32), field[PIX - TC :].astype(F32))
+        set_corners(fcor.at[t], 0, field[:TC].astype(F32))
+        set_corners(fcor.at[t], 1, field[PIX - TC :].astype(F32))
 
     @pl.when(first & kept)
     def _():
@@ -306,17 +318,16 @@
             win[TC : TC + PIX, pl.ds(2 * side * stride + base, width)] = moved
         win[TC : TC + PIX, pl.ds(stride + base, width)] = whole[:PIX]
 
-    def spread_far(buf, cor, t, width, win, base, stride):
-        whole = buf[t, NEAR:SLOTS].reshape(2 * TC, width)
+    def spread_far(low, buf, cor, t, width, win, base, stride):
+        whole = buf[t, NEAR + low]
         q_at = lax.broadcasted_iota(jnp.int32, (TC, width), 0)
         for side in range(2):
             moved = jnp.dot(pick_far[side], whole, preferred_element_type=F32)
             rim = q_at == (0 if side == 0 else TC - 1)
-            for low in range(2):
-                cell = jnp.broadcast_to(cor[t, 2 * low + side], (TC, width))
-                part = jnp.where(rim, cell, moved[low * TC : (low + 1) * TC])
-                win[low * TC : (low + 1) * TC, pl.ds(2 * side * stride + base, width)] = part.astype(BF)
-        win[:, pl.ds(stride + base, width)] = whole
+            cell = jnp.broadcast_to(cor[t, 2 * low + side], (TC, width))
+            part = jnp.where(rim, cell, moved)
+            win[low * TC : (low + 1) * TC, pl.ds(2 * side * stride + base, width)] = part.astype(BF)
+        win[low * TC : (low + 1) * TC, pl.ds(stride + base, width)] = whole
 
     cells[0] = jnp.zeros((PIX, CH), F32)
 
@@ -356,7 +367,8 @@
         @pl.when(sec > 0)
         def _():
             wait_for(xin.at[t, pl.ds(1, TR - 2)], xt_sem.at[t, 0])
-            wait_for(xin.at[t, pl.ds(0, 2)], xt_sem.at[t, 1])
+            wait_for(xin.at[t, pl.ds(0, 1)], xt_sem.at[t, 1])
+            wait_for(xin.at[t, pl.ds(0, 1)], xt_sem.at[t, 2])
 
         settle_rims(NEAR_DELTAS, xin.at[t], xcin.at[t], x_sem.at[t])
         spread(xin, t, CH, win_f, 0, 2 * CH)
@@ -374,22 +386,6 @@
         @pl.when(sec < sections - 1)
         def _():
             send_rows(hin, t + 1, xin, t, 1, TR - 2, sec + 1, xts_sem.at[t, 0], xt_sem.at[t, 0])
-
-        @pl.when(t > 0)
-        def _():
-            settle_rims(FAR_DELTAS, hin.at[t], hcin.at[t], h_sem.at[t])
-
-        settle_rims(FAR_DELTAS, xin.at[t], xcin.at[t], x_sem.at[t])
-        spread_far(hin, hcin, t, CH, far_f, CH, 2 * CH)
-        spread_far(xin, xcin, t, CH, far_f, 0, 2 * CH)
-        for a, start in ((0, 0), (2, PIX - TC)):
-            far = far_f[0:TC, :] if a == 0 else far_f[TC : 2 * TC, :]
-            z_ref[start : start + TC, :] += lax.dot_general(
-                far, wf[a], (((1,), (1,)), ((), ())), preferred_element_type=F32
-            )
-        top = advance(t, 0, TC)
-        low = advance(t, PIX - TC, PIX)
-        set_corners(hcor.at[t], top, low)
 
         def share(deltas):
             @pl.when(sec < sections - 1)
@@ -412,13 +408,31 @@
                     h_sem.at[t + 1],
                 )
 
-        share(FAR_DELTAS)
-
-        @pl.when(sec < sections - 1)
-        def _():
-            for edge_row in (0, TR - 1):
-                send_rows(hin, t + 1, xin, t, edge_row, 1, sec + 1, xts_sem.at[t, 1], xt_sem.at[t, 1])
-
+        def finish(side):
+            deltas = BELOW if side else ABOVE
+            start = side * (PIX - TC)
+
+            @pl.when(t > 0)
+            def _():
+                settle_rims(deltas, hin.at[t], hcin.at[t], h_sem.at[t])
+
+            settle_rims(deltas, xin.at[t], xcin.at[t], x_sem.at[t])
+            spread_far(side, hin, hcin, t, CH, far_f, CH, 2 * CH)
+            spread_far(side, xin, xcin, t, CH, far_f, 0, 2 * CH)
+            z_ref[start : start + TC, :] += lax.dot_general(
+                far_f[side * TC : (side + 1) * TC, :],
+                wf[2 * side],
+                (((1,), (1,)), ((), ())),
+                preferred_element_type=F32,
+            )
+            set_corners(hcor.at[t], side, advance(t, start, start + TC))
+            share(ABOVE if side else BELOW)
+
+            @pl.when(sec < sections - 1)
+            def _():
+                send_rows(hin, t + 1, xin, t, side * (TR - 1), 1, sec + 1, xts_sem.at[t, 1 + side], xt_sem.at[t, 1 + side])
+
+        both_sides(finish)
         field = hin[t + 1, 0:TR].reshape(PIX, CH)
         hcol[t] = columns(field).reshape(2, TR, CH)
         share(NEAR_DELTAS)
@@ -468,20 +482,22 @@
 
         slope(t, TC, PIX - TC)
 
-        @pl.when(sec < sections - 1)
-        def _():
-            wait_for(din.at[t, pl.ds(0, 2)], d_sem.at[t, 1])
-
-        top = slope(t, 0, TC)
-        low = slope(t, PIX - TC, PIX)
-        set_corners(zcor.at[t], top, low)
-
         def share(deltas):
             rims(
                 deltas, dzin.at[t], dzcol.at[t], zcor.at[t], dzin.at[t], zcin.at[t], sec, dzs_sem.at[t], dz_sem.at[t]
             )
 
-        share(FAR_DELTAS)
+        def begin(side):
+            start = side * (PIX - TC)
+
+            @pl.when(sec < sections - 1)
+            def _():
+                wait_for(din.at[t, pl.ds(0, 1)], d_sem.at[t, 1 + side])
+
+            set_corners(zcor.at[t], side, slope(t, start, start + TC))
+            share(ABOVE if side else BELOW)
+
+        both_sides(begin)
         dzcol[t] = columns(dzin[t, 0:TR].reshape(PIX, 4 * CH)).reshape(2, TR, 4 * CH)
         share(NEAR_DELTAS)
         emit(0, hidden_ref, t, hin[t + 1, 0:TR])
@@ -506,19 +522,21 @@
         def _():
             send_rows(*above, 1, TR - 2, sec - 1, ds_sem.at[t, 0], d_sem.at[t, 0])
 
-        settle_rims(FAR_DELTAS, dzin.at[t], zcin.at[t], dz_sem.at[t])
-        spread_far(dzin, zcin, t, 4 * CH, far_b, 0, 4 * CH)
-        for a, start in ((2, 0), (0, PIX - TC)):
-            far = far_b[0:TC, :] if a == 2 else far_b[TC : 2 * TC, :]
-            rim = du_ref[start : start + TC, :] + jnp.dot(far, wb[a], preferred_element_type=F32)
+        def finish(side):
+            start = side * (PIX - TC)
+            settle_rims(BELOW if side else ABOVE, dzin.at[t], zcin.at[t], dz_sem.at[t])
+            spread_far(side, dzin, zcin, t, 4 * CH, far_b, 0, 4 * CH)
+            rim = du_ref[start : start + TC, :] + jnp.dot(
+                far_b[side * TC : (side + 1) * TC, :], wb[2 - 2 * side], preferred_element_type=F32
+            )
             du_ref[start : start + TC, :] = rim
-            dsend[t, start // TC] = rim[:, :CH].astype(BF)
-
-        @pl.when(sec > 0)
-        def _():
-            for edge_row in (0, TR - 1):
-                send_rows(*above, edge_row, 1, sec - 1, ds_sem.at[t, 1], d_sem.at[t, 1])
-
+            dsend[t, side * (TR - 1)] = rim[:, :CH].astype(BF)
+
+            @pl.when(sec > 0)
+            def _():
+                send_rows(*above, side * (TR - 1), 1, sec - 1, ds_sem.at[t, 1 + side], d_sem.at[t, 1 + side])
+
+        both_sides(finish)
         return carry
 
     @pl.when(last)
@@ -539,7 +557,8 @@
         def _():
             settle_rims(DELTAS, xin.at[t], xcin.at[t], xs_sem.at[t], -1)
             wait_for(xin.at[t, pl.ds(1, TR - 2)], xts_sem.at[t, 0])
-            wait_for(xin.at[t, pl.ds(0, 2)], xts_sem.at[t, 1])
+            wait_for(xin.at[t, pl.ds(0, 1)], xts_sem.at[t, 1])
+            wait_for(xin.at[t, pl.ds(0, 1)], xts_sem.at[t, 2])
 
         @pl.when(t < STEPS - 1)
         def _():
@@ -550,7 +569,8 @@
         @pl.when(sec > 0)
         def _():
             wait_for(dsend.at[t, pl.ds(1, TR - 2)], ds_sem.at[t, 0])
-            wait_for(dsend.at[t, pl.ds(0, 2)], ds_sem.at[t, 1])
+            wait_for(dsend.at[t, pl.ds(0, 1)], ds_sem.at[t, 1])
+            wait_for(dsend.at[t, pl.ds(0, 1)], ds_sem.at[t, 2])
 
         return carry
 
@@ -611,7 +631,7 @@
             pltpu.VMEM((3, 4 * CH, 6 * CH), BF),
             pltpu.VMEM((3, 12 * CH, 2 * CH), BF),
             pltpu.VMEM((2, PIX, NEAR * TC), BF),
-            pltpu.VMEM((2, 2 * TC, 2 * TC), BF),
+            pltpu.VMEM((2, TC, TC), BF),
             pltpu.VMEM((2 * TR, PIX), BF),
             pltpu.VMEM((EXT, 6 * CH), BF),
             pltpu.VMEM((EXT, 12 * CH), BF),
@@ -626,14 +646,14 @@
             pltpu.SemaphoreType.DMA((STEPS, 8)),
             pltpu.SemaphoreType.DMA((STEPS, 8)),
             pltpu.SemaphoreType.DMA((STEPS, 8)),
-            pltpu.SemaphoreType.DMA((STEPS, 2)),
-            pltpu.SemaphoreType.DMA((STEPS, 2)),
+            pltpu.SemaphoreType.DMA((STEPS, 3)),
+            pltpu.SemaphoreType.DMA((STEPS, 3)),
             pltpu.SemaphoreType.DMA((STEPS, 8)),
             pltpu.SemaphoreType.DMA((STEPS, 8)),
             pltpu.SemaphoreType.DMA((STEPS, 8)),
-            pltpu.SemaphoreType.DMA((STEPS, 2)),
+            pltpu.SemaphoreType.DMA((STEPS, 3)),
             pltpu.SemaphoreType.DMA((STEPS, 8)),
-            pltpu.SemaphoreType.DMA((STEPS, 2)),
+            pltpu.SemaphoreType.DMA((STEPS, 3)),
             pltpu.SemaphoreType.DMA((2, 9)),
             pltpu.SemaphoreType.DMA((2, STEPS)),
             pltpu.SemaphoreType.DMA((2,)),

time: 167 us -> 163 us (0.976)
  Pallas kernels: 161 us -> 157 us
    pallas_call x1, Pallas kernels: 161 us -> 157 us  [per_device(): step(frames.reshape(STEPS, CH, PIX), weights[0], gate_bias, cotangent.res...]
where the time goes in v5:
time: 163 us; the launch traced here: 161 us
  Pallas kernels  157 us (96%)
  local copies, waits for them, and re-layouts  3.34 us (2%)
    pallas_call x1, Pallas kernels, per_device(): step(frames.reshape(STEPS, CH, PIX), weights[0], gate_bias, cotangent.res...  157 us
    unnamed x2, local copies, waits for them, and re-layouts  3.34 us

profile of v5, /device:TPU:6, one launch (start us, length us, event | category | flops | bytes accessed | tf_op | source)
XLA Modules:
  0.0 161.1 jit_solution(13507555531722833813)
XLA Ops:
  0.6 157.1 %conv_lstm.1 = (bf16[4,128,256]{2,1,0:T(8,128)(2,1)}, bf16[4,128,256]{2,1,0:T(8,128)(2,1)}) custom-call(bf16[4,128,256]{2,1,0:T(8,128)(2,1)} %bitcast.10, bf16[9,512,256]{2,1,0:T(8,128)(2,1)} %bitcast.9, f32[1,512]{1,0:T(1,128)} %refs_2_.1, bf16[4,128,256]{2,1,0:T(8,128)(2,1)} %bitcast.11), custom_call_target="tpu_custom_call" | custom-call | tf_op jit(solution)/shard_map/conv_lstm/pallas_call | solution.py:673
  157.7 1.7 %copy.10 = bf16[1,4,128,1,256]{4,2,3,1,0:T(8,128)(2,1)} copy(bf16[1,4,128,1,256]{4,2,3,1,0:T(8,128)(2,1)} %bitcast.13) | data formatting | bytes 524288
  159.4 1.7 %copy.11 = bf16[1,4,128,1,256]{4,2,3,1,0:T(8,128)(2,1)} copy(bf16[1,4,128,1,256]{4,2,3,1,0:T(8,128)(2,1)} %bitcast.12) | data formatting | bytes 524288

commit v6 on v5

--- a/solution.py
+++ b/solution.py
@@ -291,22 +291,17 @@
         for t in range(STEPS):
             to_partner(frames_ref.at[t], frames_in.at[t], fin_sem.at[0, t], fin_sem.at[1, t]).start()
 
-    @pl.when(swapped)
-    def _():
-        to_partner(cot_ref, cot_in, cin_sem.at[0], cin_sem.at[1]).start()
+    def enter(t):
+        @pl.when(swapped)
+        def _():
+            wait_for(frames_in.at[t], fin_sem.at[1, t])
+            place(frames_in, t)
+
+        rims(DELTAS, xin.at[t], fcol.at[t], fcor.at[t], xin.at[t], xcin.at[t], sec, fs_sem.at[t], x_sem.at[t])
 
     @pl.when(first)
     def _():
-        def share(t, carry):
-            @pl.when(swapped)
-            def _():
-                wait_for(frames_in.at[t], fin_sem.at[1, t])
-                place(frames_in, t)
-
-            rims(DELTAS, xin.at[t], fcol.at[t], fcor.at[t], xin.at[t], xcin.at[t], sec, fs_sem.at[t], x_sem.at[t])
-            return carry
-
-        lax.fori_loop(0, STEPS, share, 0)
+        enter(0)
 
     for copy in copies[0::2]:
         copy.wait()
@@ -358,6 +353,10 @@
         return hidden.astype(F32)
 
     def forward(t, carry):
+        @pl.when(first & (t < STEPS - 1))
+        def _():
+            enter(t + 1)
+
         @pl.when(t > 0)
         def _():
             settle_rims(NEAR_DELTAS, hin.at[t], hcin.at[t], h_sem.at[t])
@@ -436,6 +435,11 @@
         field = hin[t + 1, 0:TR].reshape(PIX, CH)
         hcol[t] = columns(field).reshape(2, TR, CH)
         share(NEAR_DELTAS)
+
+        @pl.when(swapped & (t == 0))
+        def _():
+            to_partner(cot_ref, cot_in, cin_sem.at[0], cin_sem.at[1]).start()
+
         return carry
 
     lax.fori_loop(0, STEPS, forward, 0)

time: 163 us -> 162 us (level)
  no operation moved by 1% of the time
where the time goes in v6:
time: 162 us; the launch traced here: 160 us
  Pallas kernels  156 us (96%)
  local copies, waits for them, and re-layouts  3.34 us (2%)
    pallas_call x1, Pallas kernels, per_device(): step(frames.reshape(STEPS, CH, PIX), weights[0], gate_bias, cotangent.res...  156 us
    unnamed x2, local copies, waits for them, and re-layouts  3.34 us

profile of v6, /device:TPU:6, one launch (start us, length us, event | category | flops | bytes accessed | tf_op | source)
XLA Modules:
  0.0 160.3 jit_solution(3412048576302067249)
XLA Ops:
  0.6 156.3 %conv_lstm.1 = (bf16[4,128,256]{2,1,0:T(8,128)(2,1)}, bf16[4,128,256]{2,1,0:T(8,128)(2,1)}) custom-call(bf16[4,128,256]{2,1,0:T(8,128)(2,1)} %bitcast.10, bf16[9,512,256]{2,1,0:T(8,128)(2,1)} %bitcast.9, f32[1,512]{1,0:T(1,128)} %refs_2_.1, bf16[4,128,256]{2,1,0:T(8,128)(2,1)} %bitcast.11), custom_call_target="tpu_custom_call" | custom-call | tf_op jit(solution)/shard_map/conv_lstm/pallas_call | solution.py:677
  157.0 1.7 %copy.10 = bf16[1,4,128,1,256]{4,2,3,1,0:T(8,128)(2,1)} copy(bf16[1,4,128,1,256]{4,2,3,1,0:T(8,128)(2,1)} %bitcast.13) | data formatting | bytes 524288
  158.7 1.7 %copy.11 = bf16[1,4,128,1,256]{4,2,3,1,0:T(8,128)(2,1)} copy(bf16[1,4,128,1,256]{4,2,3,1,0:T(8,128)(2,1)} %bitcast.12) | data formatting | bytes 524288
